TPU v7x, 512 devices: a whole 4x4x16 slice. The times are simulated.
512 devices in a mesh: long: 32 (over y, z_hi, core), aq: 16 (over x, z_lo).
Axes of the slice: x: 4, y: 4, z: 16 (z_hi: 4, z_lo: 4; z = z_hi * 4 + z_lo), core: 2. Of those that a mesh axis runs over, the one named last changes fastest.
Arguments:
- column_seed: float32 [2, 64, 256, 2048], P(None, None, 'long', 'aq'), may hold values from -6 to 6
- head_seed: float32 [256, 2048], P(None, 'aq'), may hold values from -6 to 6
- texture: int32 [64, 256, 2048], P(None, 'long', 'aq'), may hold values from 0 to 11
- soil_table: float32 [3, 12], replicated, may hold values from 0.2 to 5
- active: int32 [256, 2048], P('long', 'aq'), may hold values 0 or 1
- conductance: float32 [256, 2048], P('long', 'aq'), may hold values from 0.2 to 2
- wells: int32 [256, 2048], P('long', 'aq'), may hold values from 0 to 32767
- transmissivity: float32 [256, 2048], P(None, 'aq'), may hold values from 0.1 to 1
- storage: float32 [256, 2048], P(None, 'aq'), may hold values from 0.01 to 0.1
Outputs:
- column_adjoint: float32 [2, 64, 256, 2048], P(None, None, 'long', 'aq')
- recharge_adjoint: float32 [256, 2048], P('long', 'aq')
- head_adjoint: float32 [256, 2048], P('long', 'aq')
Inputs may be any that keep to these rules, and one draw needn't show every extreme that they name: `wells`: the well of column (x, y) lies in the aquifer cells of the same group of 128 second coordinates, with the index x' * 128 + y' mod 128.
All inputs are finite; a program needn't handle non-finite values. No bound on the sum of `active` on one device may be relied on, other than what follows from the above.
Results may differ from a plain program's by a relative error of at most 0.0001.
Values sent between devices are 32-bit elements; how exact they have to be, the bound alone decides.
A program may use at most 64 MiB of HBM per device.

v0:
```python
import jax
import jax.numpy as jnp
from jax import lax
from jax.sharding import PartitionSpec as P

SWEEPS = 4
STEPS = 2


RELAX = 0.8


def padded_2(block, sides, width):
    for axis, dim in sides:
        count = lax.axis_size(axis)
        forward = [(i, i + 1) for i in range(count - 1)]
        backward = [(target, source) for source, target in forward]
        low = lax.ppermute(
            lax.slice_in_dim(block, block.shape[dim] - width, None, axis=dim), axis, forward
        )
        high = lax.ppermute(lax.slice_in_dim(block, 0, width, axis=dim), axis, backward)
        block = jnp.concatenate([low, block, high], axis=dim)
    return block


def lookup(texture, table_row):
    values = jnp.zeros(texture.shape, jnp.float32)
    for number in range(table_row.shape[0]):
        values = jnp.where(texture == number, table_row[number], values)
    return values


def column_solve(faces, forcing):
    layer_count = forcing.shape[0]
    ratios = []
    partials = []
    for layer_index in range(layer_count):
        diagonal = jnp.ones_like(forcing[0])
        if layer_index > 0:
            diagonal = diagonal + faces[layer_index - 1]
        if layer_index < layer_count - 1:
            diagonal = diagonal + faces[layer_index]
        if layer_index == 0:
            pivot_value = diagonal
            carried = forcing[0]
        else:
            pivot_value = diagonal - faces[layer_index - 1] * ratios[-1]
            carried = forcing[layer_index] + faces[layer_index - 1] * partials[-1]
        if layer_index < layer_count - 1:
            ratios.append(faces[layer_index] / pivot_value)
        partials.append(carried / pivot_value)
    solution = [partials[-1]]
    for layer_index in range(layer_count - 2, -1, -1):
        solution.append(partials[layer_index] + ratios[layer_index] * solution[-1])
    return jnp.stack(solution[::-1])


def face_arrays(padded_t, col_start, total_rows, total_cols):
    centre = padded_t[1:-1, 1:-1]
    row_ids = lax.broadcasted_iota(jnp.int32, centre.shape, 0)
    col_ids = col_start + lax.broadcasted_iota(jnp.int32, centre.shape, 1)
    east_face = jnp.where(row_ids + 1 < total_rows, 0.5 * (centre + padded_t[2:, 1:-1]), 0.0)
    west_face = jnp.where(row_ids >= 1, 0.5 * (centre + padded_t[:-2, 1:-1]), 0.0)
    north_face = jnp.where(col_ids + 1 < total_cols, 0.5 * (centre + padded_t[1:-1, 2:]), 0.0)
    south_face = jnp.where(col_ids >= 1, 0.5 * (centre + padded_t[1:-1, :-2]), 0.0)
    return (east_face, west_face, north_face, south_face)


def relax(forcing_head, face_set, storage, neighbours):
    east_face, west_face, north_face, south_face = face_set
    diagonal = storage + east_face + west_face + north_face + south_face
    estimate = jnp.zeros_like(forcing_head)
    for sweep_number in range(SWEEPS):
        padded = neighbours(estimate)
        beside = east_face * padded[2:, 1:-1] + west_face * padded[:-2, 1:-1]
        beside = beside + north_face * padded[1:-1, 2:] + south_face * padded[1:-1, :-2]
        estimate = estimate + RELAX * (forcing_head - (diagonal * estimate - beside)) / diagonal
    return estimate


def shards(
    column_seed, head_seed, texture, soil_table, active, conductance, wells, transmissivity, storage
):
    local_rows = column_seed.shape[2]
    local_cols = column_seed.shape[3]
    total_rows = local_rows * lax.axis_size("long")
    total_cols = local_cols * lax.axis_size("aq")
    row_start = lax.axis_index("long") * local_rows
    col_start = lax.axis_index("aq") * local_cols
    water_number = lookup(texture, soil_table[0])
    heat_number = lookup(texture, soil_table[1])
    coupling = 0.2 * lookup(texture, soil_table[2])
    water_faces = 0.5 * (water_number[:-1] + water_number[1:])
    heat_faces = 0.5 * (heat_number[:-1] + heat_number[1:])
    gain = jnp.where(active == 1, conductance, 0.0)
    rimmed_t = padded_2(transmissivity, (("aq", 1),), 1)
    padded_t = jnp.pad(rimmed_t, ((1, 1), (0, 0)))
    face_set = face_arrays(padded_t, col_start, total_rows, total_cols)
    head_state = head_seed

    def neighbours(estimate):
        rimmed = padded_2(estimate, (("aq", 1),), 1)
        return jnp.pad(rimmed, ((1, 1), (0, 0)))

    def local_part(estimate):
        return lax.dynamic_slice_in_dim(estimate, row_start, local_rows, 0)

    flat_wells = wells.reshape(-1)
    water_adjoint = column_seed[0]
    heat_adjoint = column_seed[1]
    recharge = jnp.zeros((local_rows, local_cols), jnp.float32)
    for time_step in range(STEPS):
        heat_next = column_solve(heat_faces, heat_adjoint)
        estimate = relax(head_state, face_set, storage, neighbours)
        recharge = local_part(estimate)
        forcing = water_adjoint + coupling * heat_next
        forcing = jnp.concatenate([forcing[:-1], (forcing[-1] + gain * recharge)[None]], 0)
        water_next = column_solve(water_faces, forcing)
        well_term = gain * water_next[-1]
        owner_slab = (
            jnp.zeros((total_rows * local_cols,), jnp.float32)
            .at[flat_wells]
            .add(well_term.reshape(-1))
        )
        collect_owner_slab = owner_slab.reshape(total_rows, local_cols)
        head_state = estimate + lax.psum(collect_owner_slab, "long")
        water_adjoint = water_next
        heat_adjoint = heat_next
    return (jnp.stack([water_adjoint, heat_adjoint]), recharge, local_part(head_state))


def solution(mesh):
    return jax.shard_map(
        shards,
        mesh=mesh,
        in_specs=(
            P(None, None, "long", "aq"),
            P(None, "aq"),
            P(None, "long", "aq"),
            P(),
            P("long", "aq"),
            P("long", "aq"),
            P("long", "aq"),
            P(None, "aq"),
            P(None, "aq"),
        ),
        out_specs=(P(None, None, "long", "aq"), P("long", "aq"), P("long", "aq")),
        check_vma=False,
    )
```

profile of v0, /device:TPU:1, one launch (start us, length us, event | category | flops | bytes accessed | tf_op | source)
XLA Modules:
  0.0 795.6 jit_solution(4939642235235876168)
XLA Ops:
  7.2 4.5 collective-permute-start.2
  11.8 1.3 collective-permute-start.3
  13.1 0.7 fusion.1063
  13.8 1.4 collective-permute-start.1
  15.2 4.8 collective-permute-start
  20.0 0.7 fusion.1065
  20.7 0.7 fusion.1064
  21.5 7.9 select_select_fusion
  29.4 7.9 select_select_fusion.1
  37.4 0.9 copy-done.1
  38.4 0.3 fusion.491
  38.8 0.3 fusion.368
  39.1 0.2 fusion.418
  39.3 0.2 constant_dynamic-update-slice_fusion.63
  39.6 0.5 constant_dynamic-update-slice_fusion.62
  40.7 0.4 fusion.425
  41.1 0.4 constant_dynamic-update-slice_fusion.191
  41.7 0.6 constant_dynamic-update-slice_fusion.189
  43.0 7.7 bitcast_add_fusion
  51.2 0.7 copy-done
  52.0 0.4 multiply_divide_fusion.1
  52.5 3.5 collective-permute-start.4
  56.0 1.3 collective-permute-start.5
  57.6 0.3 collective-permute-done.4
  58.0 3.8 collective-permute-done.5
  61.9 0.3 fusion.64
  62.3 8.0 %collective-permute-start.6 = (f32[256,1]{1,0:T(8,128)S(1)}, f32[256,1]{1,0:T(8,128)S(1)}, u32[]{:S(2)}, u32[]{:S(2)}) collective-permute-start(f32[256,1]{1,0:T(8,128)S(1)} %get-tuple-element.687), channel_id=1, source_target_pairs={{0,1},{1,2},{2,3},{3,4},{4,5},{5,6},{6,7},{7,8},{8,9},{9,10},{10,1... | collective-permute-start | bytes 3080 | tf_op jit(solution)/shard_map/ppermute | solution.py:18
  70.3 1.3 collective-permute-start.7
  71.7 0.8 fusion.303
  72.5 5.0 collective-permute-done.7
  77.7 0.3 fusion.54
  78.1 1.7 collective-permute-start.8
  79.9 1.3 collective-permute-start.9
  81.2 0.6 compare_select_fusion
  81.8 5.9 collective-permute-done.9
  87.9 0.3 fusion.44
  88.1 0.4 copy-done.67
  88.5 0.9 multiply_bitcast_fusion.1
  89.7 0.5 copy-done.63
  91.3 6.7 scatter_custom_fusion
  98.1 329.8 %all-reduce.13.cloned.1.call-done = f32[256,128]{1,0:T(8,128)} async-done(((f32[256,128]{1,0:T(8,128)}), f32[256,128]{1,0:T(8,128)}) %all-reduce.13.cloned.1.call-update) | async-done | bytes 131088 | tf_op jit(solution)/shard_map/psum | solution.py:126
  427.9 1.1 multiply_divide_fusion
  429.1 2.3 collective-permute-start.10
  431.4 1.3 collective-permute-start.11
  432.7 0.6 collective-permute-done.10
  433.3 7.6 collective-permute-done.11
  441.0 0.3 fusion.34
  441.4 2.0 collective-permute-start.12
  443.4 1.5 collective-permute-start.13
  444.9 0.4 collective-permute-done.12
  445.3 7.3 collective-permute-done.13
  452.8 0.3 fusion.24
  453.1 2.8 collective-permute-start.14
  455.9 1.3 collective-permute-start.15
  457.3 0.6 collective-permute-done.14
  457.8 7.2 collective-permute-done.15
  465.5 0.3 fusion.14
  466.1 0.3 copy-done.11
  466.4 0.2 multiply_bitcast_fusion
  466.6 0.2 constant_dynamic-update-slice_fusion.255
  467.6 6.7 scatter_custom_fusion.1
  474.3 0.8 pad_maximum_fusion
  475.2 312.4 %all-reduce.15.cloned.1.call-done = f32[256,128]{1,0:T(8,128)} async-done(((f32[256,128]{1,0:T(8,128)}), f32[256,128]{1,0:T(8,128)}) %all-reduce.15.cloned.1.call-update) | async-done | bytes 131088 | tf_op jit(solution)/shard_map/psum | solution.py:126
  787.5 1.3 dynamic-slice_add_fusion
  (420 shorter events, 4.9 us)
Async XLA Ops:
  7.2 5.9 copy-start.3
  7.2 420.7 %all-reduce.13.cloned.1.call-start = ((), (), s32[]{:S(2)}) async-start(), calls=%async_computation | async-start | bytes 262144 | tf_op jit(solution)/shard_map/psum | solution.py:126
  7.2 14.2 %copy-start.4 = (s32[64,8,128]{2,1,0:T(8,128)S(1)}, s32[64,8,128]{2,1,0:T(8,128)}, u32[]{:S(2)}) copy-start(s32[64,8,128]{2,1,0:T(8,128)} %param.11) | copy-start | bytes 786436
  7.2 43.7 %collective-permute-start.2 = (f32[256,1]{1,0:T(8,128)S(1)}, f32[256,1]{1,0:T(8,128)S(1)}, u32[]{:S(2)}, u32[]{:S(2)}) collective-permute-start(f32[256,1]{1,0:T(8,128)S(1)} %broadcast.5304), channel_id=1, source_target_pairs={{0,1},{1,2},{2,3},{3,4},{4,5},{5,6},{6,7},{7,8},{8,9},{9,10},{10,1... | collective-permute-start | bytes 3080 | tf_op jit(solution)/shard_map/ppermute | solution.py:18
  11.8 39.2 %collective-permute-start.3 = (f32[256,1]{1,0:T(8,128)S(1)}, f32[256,1]{1,0:T(8,128)S(1)}, u32[]{:S(2)}, u32[]{:S(2)}) collective-permute-start(f32[256,1]{1,0:T(8,128)S(1)} %broadcast.5304), channel_id=1, source_target_pairs={{1,0},{2,1},{3,2},{4,3},{5,4},{6,5},{7,6},{8,7},{9,8},{10,9},{11,1... | collective-permute-start | bytes 3080 | tf_op jit(solution)/shard_map/ppermute | solution.py:21
  13.8 6.2 copy-start.5
  13.8 37.0 %collective-permute-start.1 = (f32[256,1]{1,0:T(8,128)}, f32[256,1]{1,0:T(8,128)S(1)}, u32[]{:S(2)}, u32[]{:S(2)}) collective-permute-start(f32[256,1]{1,0:T(8,128)} %get-tuple-element.691), channel_id=1, source_target_pairs={{1,0},{2,1},{3,2},{4,3},{5,4},{6,5},{7,6},{8,7},{9,8},{10,9},{11,1... | collective-permute-start | bytes 3080 | tf_op jit(solution)/shard_map/ppermute | solution.py:21
  15.2 35.6 %collective-permute-start = (f32[256,1]{1,0:T(8,128)S(1)}, f32[256,1]{1,0:T(8,128)S(1)}, u32[]{:S(2)}, u32[]{:S(2)}) collective-permute-start(f32[256,1]{1,0:T(8,128)S(1)} %get-tuple-element.690), channel_id=1, source_target_pairs={{0,1},{1,2},{2,3},{3,4},{4,5},{5,6},{6,7},{7,8},{8,9},{9,10},{10,1... | collective-permute-start | bytes 3080 | tf_op jit(solution)/shard_map/ppermute | solution.py:18
  37.3 1.0 copy-start.1
  51.0 0.9 copy-start
  51.0 1.0 copy-start.2
  52.5 5.5 collective-permute-start.4
  56.0 5.7 collective-permute-start.5
  57.5 14.1 %copy-start.6 = (f32[8,128]{1,0:T(8,128)}, f32[8,128]{1,0:T(8,128)S(1)}, u32[]{:S(2)}) copy-start(f32[8,128]{1,0:T(8,128)S(1)} %get-tuple-element.249) | copy-start | bytes 12292
  57.5 14.1 %copy-start.8 = (f32[8,128]{1,0:T(8,128)}, f32[8,128]{1,0:T(8,128)S(1)}, u32[]{:S(2)}) copy-start(f32[8,128]{1,0:T(8,128)S(1)} %get-tuple-element.252) | copy-start | bytes 12292
  57.6 14.1 %copy-start.10 = (f32[8,128]{1,0:T(8,128)}, f32[8,128]{1,0:T(8,128)S(1)}, u32[]{:S(2)}) copy-start(f32[8,128]{1,0:T(8,128)S(1)} %get-tuple-element.255) | copy-start | bytes 12292
  57.6 14.1 %copy-start.12 = (f32[8,128]{1,0:T(8,128)}, f32[8,128]{1,0:T(8,128)S(1)}, u32[]{:S(2)}) copy-start(f32[8,128]{1,0:T(8,128)S(1)} %get-tuple-element.258) | copy-start | bytes 12292
  57.6 14.1 %copy-start.14 = (f32[8,128]{1,0:T(8,128)}, f32[8,128]{1,0:T(8,128)S(1)}, u32[]{:S(2)}) copy-start(f32[8,128]{1,0:T(8,128)S(1)} %get-tuple-element.261) | copy-start | bytes 12292
  57.6 14.1 %copy-start.16 = (f32[8,128]{1,0:T(8,128)}, f32[8,128]{1,0:T(8,128)S(1)}, u32[]{:S(2)}) copy-start(f32[8,128]{1,0:T(8,128)S(1)} %get-tuple-element.264) | copy-start | bytes 12292
  57.6 14.1 %copy-start.18 = (f32[8,128]{1,0:T(8,128)}, f32[8,128]{1,0:T(8,128)S(1)}, u32[]{:S(2)}) copy-start(f32[8,128]{1,0:T(8,128)S(1)} %get-tuple-element.267) | copy-start | bytes 12292
  57.6 14.1 %copy-start.20 = (f32[8,128]{1,0:T(8,128)}, f32[8,128]{1,0:T(8,128)S(1)}, u32[]{:S(2)}) copy-start(f32[8,128]{1,0:T(8,128)S(1)} %get-tuple-element.270) | copy-start | bytes 12292
  57.6 14.1 %copy-start.22 = (f32[8,128]{1,0:T(8,128)}, f32[8,128]{1,0:T(8,128)S(1)}, u32[]{:S(2)}) copy-start(f32[8,128]{1,0:T(8,128)S(1)} %get-tuple-element.273) | copy-start | bytes 12292
  62.3 10.2 %collective-permute-start.6 = (f32[256,1]{1,0:T(8,128)S(1)}, f32[256,1]{1,0:T(8,128)S(1)}, u32[]{:S(2)}, u32[]{:S(2)}) collective-permute-start(f32[256,1]{1,0:T(8,128)S(1)} %get-tuple-element.687), channel_id=1, source_target_pairs={{0,1},{1,2},{2,3},{3,4},{4,5},{5,6},{6,7},{7,8},{8,9},{9,10},{10,1... | collective-permute-start | bytes 3080 | tf_op jit(solution)/shard_map/ppermute | solution.py:18
  70.3 7.2 collective-permute-start.7
  78.1 3.1 copy-start.69
  78.1 3.7 collective-permute-start.8
  79.9 7.8 collective-permute-start.9
  87.8 0.7 copy-start.67
  87.8 0.7 copy-start.68
  89.5 0.7 copy-start.28
  89.5 0.7 copy-start.30
  89.5 0.7 copy-start.32
  89.6 0.7 copy-start.55
  89.6 0.7 copy-start.56
  89.6 0.7 copy-start.57
  89.6 0.7 copy-start.58
  89.6 0.7 copy-start.59
  89.6 0.7 copy-start.61
  89.6 0.7 copy-start.62
  89.7 0.7 copy-start.26
  89.7 0.7 copy-start.25
  89.7 0.7 copy-start.24
  98.0 689.5 %all-reduce.15.cloned.1.call-start = ((), (), s32[]{:S(2)}) async-start(), calls=%async_computation.1 | async-start | bytes 262144 | tf_op jit(solution)/shard_map/psum | solution.py:126
  429.1 4.2 collective-permute-start.10
  431.4 9.5 %collective-permute-start.11 = (f32[256,1]{1,0:T(8,128)S(1)}, f32[256,1]{1,0:T(8,128)S(1)}, u32[]{:S(2)}, u32[]{:S(2)}) collective-permute-start(f32[256,1]{1,0:T(8,128)S(1)} %get-tuple-element.682), channel_id=1, source_target_pairs={{1,0},{2,1},{3,2},{4,3},{5,4},{6,5},{7,6},{8,7},{9,8},{10,9},{11,1... | collective-permute-start | bytes 3080 | tf_op jit(solution)/shard_map/ppermute | solution.py:21
  441.4 3.9 collective-permute-start.12
  443.4 9.2 %collective-permute-start.13 = (f32[256,1]{1,0:T(8,128)S(1)}, f32[256,1]{1,0:T(8,128)S(1)}, u32[]{:S(2)}, u32[]{:S(2)}) collective-permute-start(f32[256,1]{1,0:T(8,128)S(1)} %get-tuple-element.680), channel_id=1, source_target_pairs={{1,0},{2,1},{3,2},{4,3},{5,4},{6,5},{7,6},{8,7},{9,8},{10,9},{11,1... | collective-permute-start | bytes 3080 | tf_op jit(solution)/shard_map/ppermute | solution.py:21
  453.1 4.7 collective-permute-start.14
  455.9 9.1 %collective-permute-start.15 = (f32[256,1]{1,0:T(8,128)S(1)}, f32[256,1]{1,0:T(8,128)S(1)}, u32[]{:S(2)}, u32[]{:S(2)}) collective-permute-start(f32[256,1]{1,0:T(8,128)S(1)} %get-tuple-element.678), channel_id=1, source_target_pairs={{1,0},{2,1},{3,2},{4,3},{5,4},{6,5},{7,6},{8,7},{9,8},{10,9},{11,1... | collective-permute-start | bytes 3080 | tf_op jit(solution)/shard_map/ppermute | solution.py:21
  465.2 0.7 copy-start.13
  465.2 0.7 copy-start.19
  465.2 0.7 copy-start.34
  465.3 0.7 copy-start.36
  465.3 0.7 copy-start.37
  465.3 0.7 copy-start.38
  465.3 0.7 copy-start.42
  465.3 0.7 copy-start.44
  465.4 0.7 copy-start.45
  465.4 0.7 copy-start.49
  465.4 0.7 copy-start.52
  465.4 0.7 copy-start.53
  465.4 0.7 copy-start.54
  465.7 0.7 copy-start.11
  466.6 320.9 %copy-start.66 = (f32[8,128]{1,0:T(8,128)}, f32[8,128]{1,0:T(8,128)S(1)}, u32[]{:S(2)}) copy-start(f32[8,128]{1,0:T(8,128)S(1)} %get-tuple-element.5) | copy-start | bytes 12292
  (24 other events, 16.3 us)
Sparse Core Ops, SparseCore 0:
  98.1 329.7 all-reduce.12
  474.4 313.0 all-reduce.14
where the time goes:
time: 797 us; the launch traced here: 796 us
  waiting for transfers between devices  681 us (85%)
  other arithmetic  50.6 us (6%)
  starting transfers between devices  40.4 us (5%)
  between operations  17 us (2%)
    psum x2, waiting for transfers between devices, shards(): head_state = estimate + lax.psum(collect_owner_slab, 'long')  642 us
    ppermute x8, waiting for transfers between devices, padded_2(): lax.ppermute(lax.slice_in_dim(block, 0, width, axis=dim), axis, backward)  36.7 us
    ppermute x8, starting transfers between devices, padded_2(): lax.ppermute(lax.slice_in_dim(block, block.shape[dim] - width, None, axis...  29.7 us
  transfers between devices with their start and end apart: 18, of which 12 were waited for; matrix products, arithmetic and copies ran while one was open for 4% of the time, Pallas kernels for 0%

commit v1 on v0

v1 whole, which is shorter than its diff:
```python
import jax
import jax.numpy as jnp
from jax import lax
from jax.sharding import PartitionSpec as P

SWEEPS = 4
STEPS = 2
HALO = SWEEPS

RELAX = 0.8


def aq_halo(block, width):
    count = lax.axis_size("aq")
    forward = [(i, i + 1) for i in range(count - 1)]
    backward = [(target, source) for source, target in forward]
    low = lax.ppermute(block[..., block.shape[-1] - width:], "aq", forward)
    high = lax.ppermute(block[..., :width], "aq", backward)
    return jnp.concatenate([low, block, high], axis=-1)


def lookup(texture, table_row):
    values = jnp.zeros(texture.shape, jnp.float32)
    for number in range(table_row.shape[0]):
        values = jnp.where(texture == number, table_row[number], values)
    return values


def column_solve(faces, forcing):
    layer_count = forcing.shape[0]
    ratios = []
    partials = []
    for layer_index in range(layer_count):
        diagonal = jnp.ones_like(forcing[0])
        if layer_index > 0:
            diagonal = diagonal + faces[layer_index - 1]
        if layer_index < layer_count - 1:
            diagonal = diagonal + faces[layer_index]
        if layer_index == 0:
            pivot_value = diagonal
            carried = forcing[0]
        else:
            pivot_value = diagonal - faces[layer_index - 1] * ratios[-1]
            carried = forcing[layer_index] + faces[layer_index - 1] * partials[-1]
        if layer_index < layer_count - 1:
            ratios.append(faces[layer_index] / pivot_value)
        partials.append(carried / pivot_value)
    solution = [partials[-1]]
    for layer_index in range(layer_count - 2, -1, -1):
        solution.append(partials[layer_index] + ratios[layer_index] * solution[-1])
    return jnp.stack(solution[::-1])


def relax(forcing_head, face_set, diagonal):
    east_face, west_face, north_face, south_face = face_set
    estimate = jnp.zeros_like(forcing_head)
    for sweep_number in range(SWEEPS):
        padded = jnp.pad(estimate, 1)
        beside = east_face * padded[2:, 1:-1] + west_face * padded[:-2, 1:-1]
        beside = beside + north_face * padded[1:-1, 2:] + south_face * padded[1:-1, :-2]
        estimate = estimate + RELAX * (forcing_head - (diagonal * estimate - beside)) / diagonal
    return estimate


def reduce_rows(slab, window, step):
    count = lax.axis_size("long")
    rows, cols = slab.shape
    edge = (window - step) // 2
    padded = jnp.pad(slab, ((edge, edge), (0, 0)))
    blocks = padded.reshape(-1, step, cols)
    parts = [blocks[k: k + count] for k in range(window // step)]
    chunks = jnp.stack(parts, axis=1).reshape(count, window, cols)
    got = lax.all_to_all(chunks, "long", 0, 0, tiled=True)
    return jnp.sum(got, axis=0)


def shards(
    column_seed, head_seed, texture, soil_table, active, conductance, wells, transmissivity, storage
):
    local_rows = column_seed.shape[2]
    local_cols = column_seed.shape[3]
    total_rows = local_rows * lax.axis_size("long")
    total_cols = local_cols * lax.axis_size("aq")
    row_start = lax.axis_index("long") * local_rows
    col_start = lax.axis_index("aq") * local_cols
    water_number = lookup(texture, soil_table[0])
    heat_number = lookup(texture, soil_table[1])
    coupling = 0.2 * lookup(texture, soil_table[2])
    water_faces = 0.5 * (water_number[:-1] + water_number[1:])
    heat_faces = 0.5 * (heat_number[:-1] + heat_number[1:])
    gain = jnp.where(active == 1, conductance, 0.0)

    fields = aq_halo(jnp.stack([head_seed, transmissivity, storage]), HALO)
    fields = jnp.pad(fields, ((0, 0), (HALO, HALO), (0, 0)))
    head_ext, trans_ext, storage_ext = fields[0], fields[1], fields[2]
    ext_rows, ext_cols = head_ext.shape
    row_ids = lax.broadcasted_iota(jnp.int32, (ext_rows, ext_cols), 0) - HALO
    col_ids = col_start - HALO + lax.broadcasted_iota(jnp.int32, (ext_rows, ext_cols), 1)
    valid = (row_ids >= 0) & (row_ids < total_rows) & (col_ids >= 0) & (col_ids < total_cols)
    tp = jnp.pad(trans_ext, 1)
    centre = tp[1:-1, 1:-1]
    east_face = jnp.where(valid & (row_ids + 1 < total_rows), 0.5 * (centre + tp[2:, 1:-1]), 0.0)
    west_face = jnp.where(valid & (row_ids >= 1), 0.5 * (centre + tp[:-2, 1:-1]), 0.0)
    north_face = jnp.where(valid & (col_ids + 1 < total_cols), 0.5 * (centre + tp[1:-1, 2:]), 0.0)
    south_face = jnp.where(valid & (col_ids >= 1), 0.5 * (centre + tp[1:-1, :-2]), 0.0)
    diagonal = storage_ext + east_face + west_face + north_face + south_face
    diagonal = jnp.where(valid, diagonal, 1.0)
    face_set = (east_face, west_face, north_face, south_face)

    window = local_rows + 2 * HALO

    def window_of(a):
        return lax.dynamic_slice_in_dim(a, row_start, window, 0)

    face_win = tuple(window_of(f) for f in face_set)
    diag_win = window_of(diagonal)

    flat_wells = wells.reshape(-1)

    def well_slab(water_bottom):
        well_term = gain * water_bottom
        owner_slab = (
            jnp.zeros((total_rows * local_cols,), jnp.float32)
            .at[flat_wells]
            .add(well_term.reshape(-1))
        )
        return owner_slab.reshape(total_rows, local_cols)

    core = slice(HALO, HALO + local_rows), slice(HALO, HALO + local_cols)

    heat_1 = column_solve(heat_faces, column_seed[1])
    estimate_1 = relax(head_ext, face_set, diagonal)
    recharge_1_win = window_of(estimate_1)[:, HALO:HALO + local_cols]
    recharge_1 = recharge_1_win[HALO:HALO + local_rows]
    forcing = column_seed[0] + coupling * heat_1
    forcing = jnp.concatenate([forcing[:-1], (forcing[-1] + gain * recharge_1)[None]], 0)
    water_1 = column_solve(water_faces, forcing)
    head_1_win = recharge_1_win + reduce_rows(well_slab(water_1[-1]), window, local_rows)

    heat_2 = column_solve(heat_faces, heat_1)
    head_1_ext = aq_halo(head_1_win, HALO)
    estimate_2 = relax(head_1_ext, face_win, diag_win)
    recharge_2 = estimate_2[core]
    forcing = water_1 + coupling * heat_2
    forcing = jnp.concatenate([forcing[:-1], (forcing[-1] + gain * recharge_2)[None]], 0)
    water_2 = column_solve(water_faces, forcing)
    head_2 = recharge_2 + reduce_rows(well_slab(water_2[-1]), local_rows, local_rows)
    return (jnp.stack([water_2, heat_2]), recharge_2, head_2)


def solution(mesh):
    return jax.shard_map(
        shards,
        mesh=mesh,
        in_specs=(
            P(None, None, "long", "aq"),
            P(None, "aq"),
            P(None, "long", "aq"),
            P(),
            P("long", "aq"),
            P("long", "aq"),
            P("long", "aq"),
            P(None, "aq"),
            P(None, "aq"),
        ),
        out_specs=(P(None, None, "long", "aq"), P("long", "aq"), P("long", "aq")),
        check_vma=False,
    )
```

time: 797 us -> 135 us (0.17)
  the two profiles are of different devices: /device:TPU:1 before, /device:TPU:5 now
where the time goes in v1:
time: 135 us; the launch traced here: 134 us
  other arithmetic  49.1 us (36%)
  starting transfers between devices  41.3 us (31%)
  waiting for transfers between devices  33.8 us (25%)
  local copies, waits for them, and re-layouts  6.56 us (5%)
  between operations  3.32 us (2%)
    all_to_all x2, waiting for transfers between devices, reduce_rows(): got = lax.all_to_all(chunks, 'long', 0, 0, tiled=True)  33.2 us
    all_to_all x2, starting transfers between devices, reduce_rows(): got = lax.all_to_all(chunks, 'long', 0, 0, tiled=True)  25 us
    select_n x2, other arithmetic, lookup(): values = jnp.where(texture == number, table_row[number], values)  15.8 us
    scatter-add x2, other arithmetic, well_slab(): owner_slab = jnp.zeros((total_rows * local_cols,), jnp.float32).at[flat_w...  12.5 us
    ppermute x2, starting transfers between devices, aq_halo(): high = lax.ppermute(block[..., :width], 'aq', backward)  9.39 us
    add x1, other arithmetic, shards(): forcing = column_seed[0] + coupling * heat_1  7.75 us
    ppermute x2, starting transfers between devices, aq_halo(): low = lax.ppermute(block[..., block.shape[-1] - width:], 'aq', forward)  6.91 us
    unnamed x279, local copies, waits for them, and re-layouts  4.79 us
  transfers between devices with their start and end apart: 6, of which 3 were waited for; matrix products, arithmetic and copies ran while one was open for 24% of the time, Pallas kernels for 0%

profile of v1, /device:TPU:5, one launch (start us, length us, event | category | flops | bytes accessed | tf_op | source)
XLA Modules:
  0.0 134.1 jit_solution(1031392405658463207)
XLA Ops:
  0.6 1.1 pad_maximum_fusion.1
  1.7 0.2 fusion.1056
  1.9 3.5 %collective-permute-start = (f32[3,256,4]{2,1,0:T(8,128)S(1)}, f32[3,256,4]{2,1,0:T(8,128)S(1)}, u32[]{:S(2)}, u32[]{:S(2)}) collective-permute-start(f32[3,256,4]{2,1,0:T(8,128)S(1)} %get-tuple-element.679), channel_id=1, source_target_pairs={{0,1},{1,2},{2,3},{3,4},{4,5},{5,6},{6,7},{7,8},{8,9},{9,10},{10,1... | collective-permute-start | bytes 36872 | tf_op jit(solution)/shard_map/ppermute | solution.py:17
  5.4 4.6 %collective-permute-start.1 = (f32[3,256,4]{2,1,0:T(8,128)S(1)}, f32[3,256,4]{2,1,0:T(8,128)}, u32[]{:S(2)}, u32[]{:S(2)}) collective-permute-start(f32[3,256,4]{2,1,0:T(8,128)S(1)} %get-tuple-element.680), channel_id=1, source_target_pairs={{1,0},{2,1},{3,2},{4,3},{5,4},{6,5},{7,6},{8,7},{9,8},{10,9},{11,1... | collective-permute-start | bytes 36872 | tf_op jit(solution)/shard_map/ppermute | solution.py:18
  10.1 0.6 copy-done.5
  10.8 0.7 fusion.1058
  11.5 0.7 fusion.1059
  12.2 8.0 %select_select_fusion = (f32[64,8,128]{2,1,0:T(8,128)S(1)}, pred[64,8,128]{2,1,0:T(8,128)(4,1)S(1)}, pred[64,8,128]{2,1,0:T(8,128)(4,1)S(1)}, pred[64,8,128]{2,1...) fusion(f32[]{:T(128)} %bitcast.250, ...), kind=kLoop, calls=%fused_computation.312 | loop fusion | flops 1572864 | bytes 1310768 | tf_op jit(solution)/shard_map/jit(_where)/select_n | solution.py:25
  20.2 7.8 %select_select_fusion.1 = f32[64,8,128]{2,1,0:T(8,128)S(1)} fusion(pred[64,8,128]{2,1,0:T(8,128)(4,1)S(1)} %get-tuple-element.391, pred[64,8,128]{2,1,0:T(8,128)(4,1)S(1)} %get-tuple-element.390, pred[64,8,128]{2,1,0:T(8,128)(4,1)S(1)} %get-tuple-element.389, pred[64,8,128]{2,1,0:T(8,128)(4,1)S(1)} %get-tuple-element.388, ...), kind=kLoop, calls=%fused_computation.313 | loop fusion | flops 786432 | bytes 1048624 | tf_op jit(solution)/shard_map/jit(_where)/select_n | solution.py:25
  28.1 0.9 copy-done
  29.1 0.1 fusion.613
  29.2 0.3 fusion.486
  29.5 0.3 fusion.363
  29.8 0.2 fusion.413
  30.1 0.2 constant_dynamic-update-slice_fusion.63
  30.3 0.4 fusion.420
  30.7 0.4 constant_dynamic-update-slice_fusion.191
  31.1 0.5 constant_dynamic-update-slice_fusion.62
  31.5 0.2 add_divide_fusion.11
  31.7 0.6 constant_dynamic-update-slice_fusion.189
  33.8 0.2 fusion.677
  34.1 0.4 copy-done.63
  34.5 7.8 %bitcast_add_fusion = (f32[64,8,128]{2,1,0:T(8,128)S(1)}, f32[64,8,128]{2,1,0:T(8,128)S(1)}) fusion(f32[64,8,128]{2,1,0:T(8,128)S(1)} %constant_dynamic-update-slice_fusion, f32[2,64,8,128]{3,2,1,0:T(8,128)S(1)} %copy-done, pred[64,8,128]{2,1,0:T(8,128)(4,1)S(1)} %get-tuple-element.391, pred[64,8,128]{2,1,0:T(8,128)(4,1)S(1)} %get-tuple-element.390, ...), kind=kLoop, calls=%fused_computation.310 | loop fusion | flops 983040 | bytes 1835056 | tf_op jit(solution)/shard_map/add | solution.py:135
  42.3 0.8 fusion.298
  43.1 0.1 copy-done.1
  43.2 0.1 copy-done.2
  43.3 1.4 %select_maximum_fusion = f32[3,264,136]{2,1,0:T(8,128)S(1)} fusion(f32[3,256,4]{2,1,0:T(8,128)} %collective-permute-done.1, f32[3,256,4]{2,1,0:T(8,128)S(1)} %collective-permute-done, f32[1,256,128]{2,1,0:T(8,128)S(1)} %bitcast.7745, f32[1,256,128]{2,1,0:T(8,128)S(1)} %bitcast.7747, f32[1,256,128]{2,1,0:T(8,128)S(1)} %bitcast.7749), kind=kLoop, calls=%fused_computation.4 | loop fusion | flops 1292544 | bytes 848640 | tf_op jit(solution)/shard_map/concatenate | solution.py:19
  44.7 0.6 fusion.8
  45.3 0.3 divide_add_fusion.1
  45.6 0.3 divide_add_fusion
  45.9 0.2 multiply_add_fusion
  46.2 0.6 copy-done.61
  46.8 1.0 multiply_bitcast_fusion.1
  47.8 6.0 %scatter_custom_fusion = f32[32768]{0:T(1024)S(1)} fusion(s32[1024]{0:T(1024)S(1)} %bitcast.7752, f32[1024]{0:T(1024)S(1)} %get-tuple-element.102, f32[]{:T(128)} %constant.39.clone.1), kind=kCustom, calls=%fused_computation.335 | custom fusion | flops 1024 | bytes 131076 | tf_op jit(solution)/shard_map/scatter-add | solution.py:125
  53.8 0.7 maximum_bitcast_fusion
  54.5 18.9 %all-to-all-start = ((f32[32,16,128]{2,1,0:T(8,128)}), f32[32,16,128]{2,1,0:T(8,128)S(1)}, u32[]{:S(2)}, u32[]{:S(2)}) async-start(f32[32,16,128]{2,1,0:T(8,128)} %maximum_bitcast_fusion), calls=%async_computation | async-start | bytes 524288 | tf_op jit(solution)/shard_map/all_to_all | solution.py:73
  73.9 0.3 copy-done.23
  74.1 0.0 copy-done.25
  74.3 0.0 copy-done.40
  74.3 0.0 copy-done.57
  74.4 0.0 copy-done.49
  74.5 0.0 copy-done.20
  74.5 0.2 constant_dynamic-update-slice_fusion.127
  75.5 18.9 %all-to-all-done = f32[32,16,128]{2,1,0:T(8,128)S(1)} async-done(((f32[32,16,128]{2,1,0:T(8,128)}), f32[32,16,128]{2,1,0:T(8,128)S(1)}, u32[]{:S(2)}, u32[]{:S(2)}) %all-to-all-start) | async-done | bytes 262176 | tf_op jit(solution)/shard_map/all_to_all | solution.py:73
  94.4 0.1 slice_add_fusion.2
  94.5 0.1 fusion.1057
  94.6 3.4 %collective-permute-start.2 = (f32[16,4]{1,0:T(8,128)S(1)}, f32[16,4]{1,0:T(8,128)S(1)}, u32[]{:S(2)}, u32[]{:S(2)}) collective-permute-start(f32[16,4]{1,0:T(8,128)S(1)} %get-tuple-element.689), channel_id=1, source_target_pairs={{0,1},{1,2},{2,3},{3,4},{4,5},{5,6},{6,7},{7,8},{8,9},{9,10},{10,1... | collective-permute-start | bytes 776 | tf_op jit(solution)/shard_map/ppermute | solution.py:17
  98.0 4.8 %collective-permute-start.3 = (f32[16,4]{1,0:T(8,128)S(1)}, f32[16,4]{1,0:T(8,128)S(1)}, u32[]{:S(2)}, u32[]{:S(2)}) collective-permute-start(f32[16,4]{1,0:T(8,128)S(1)} %get-tuple-element.690), channel_id=1, source_target_pairs={{1,0},{2,1},{3,2},{4,3},{5,4},{6,5},{7,6},{8,7},{9,8},{10,9},{11,1... | collective-permute-start | bytes 776 | tf_op jit(solution)/shard_map/ppermute | solution.py:18
  102.8 0.1 multiply_add_fusion.1
  102.8 0.5 collective-permute-done.3
  103.3 0.1 fusion.66
  103.4 0.1 fusion.37
  103.6 0.1 fusion.49
  103.6 0.1 fusion.55
  103.7 0.5 copy-done.13
  104.2 0.2 copy-done.11
  104.4 0.0 copy-done.9
  104.4 0.2 multiply_bitcast_fusion
  104.7 6.5 %scatter_custom_fusion.1 = f32[32768]{0:T(1024)} fusion(s32[1024]{0:T(1024)S(1)} %bitcast.7753, f32[1024]{0:T(1024)S(1)} %get-tuple-element.3, f32[]{:T(128)} %constant.39.clone.1), kind=kCustom, calls=%fused_computation.333 | custom fusion | flops 1024 | bytes 131076 | tf_op jit(solution)/shard_map/scatter-add | solution.py:125
  111.2 6.1 %all-to-all-start.1 = ((f32[32,8,128]{2,1,0:T(8,128)}), f32[32,8,128]{2,1,0:T(8,128)S(1)}, u32[]{:S(2)}, u32[]{:S(2)}) async-start(f32[32,8,128]{2,1,0:T(8,128)} %bitcast.609), calls=%async_computation.1 | async-start | bytes 262144 | tf_op jit(solution)/shard_map/all_to_all | solution.py:73
  117.3 0.2 constant_dynamic-update-slice_fusion.255
  118.3 0.8 pad_maximum_fusion
  119.1 14.3 %all-to-all-done.1 = f32[32,8,128]{2,1,0:T(8,128)S(1)} async-done(((f32[32,8,128]{2,1,0:T(8,128)}), f32[32,8,128]{2,1,0:T(8,128)S(1)}, u32[]{:S(2)}, u32[]{:S(2)}) %all-to-all-start.1) | async-done | bytes 131104 | tf_op jit(solution)/shard_map/all_to_all | solution.py:73
  133.5 0.6 add.22522
  (380 shorter events, 1.9 us)
Async XLA Ops:
  1.7 10.5 %copy-start.4 = (s32[64,8,128]{2,1,0:T(8,128)S(1)}, s32[64,8,128]{2,1,0:T(8,128)}, u32[]{:S(2)}) copy-start(s32[64,8,128]{2,1,0:T(8,128)} %param.11) | copy-start | bytes 786436
  1.9 41.2 %collective-permute-start = (f32[3,256,4]{2,1,0:T(8,128)S(1)}, f32[3,256,4]{2,1,0:T(8,128)S(1)}, u32[]{:S(2)}, u32[]{:S(2)}) collective-permute-start(f32[3,256,4]{2,1,0:T(8,128)S(1)} %get-tuple-element.679), channel_id=1, source_target_pairs={{0,1},{1,2},{2,3},{3,4},{4,5},{5,6},{6,7},{7,8},{8,9},{9,10},{10,1... | collective-permute-start | bytes 36872 | tf_op jit(solution)/shard_map/ppermute | solution.py:17
  5.4 37.7 %collective-permute-start.1 = (f32[3,256,4]{2,1,0:T(8,128)S(1)}, f32[3,256,4]{2,1,0:T(8,128)}, u32[]{:S(2)}, u32[]{:S(2)}) collective-permute-start(f32[3,256,4]{2,1,0:T(8,128)S(1)} %get-tuple-element.680), channel_id=1, source_target_pairs={{1,0},{2,1},{3,2},{4,3},{5,4},{6,5},{7,6},{8,7},{9,8},{10,9},{11,1... | collective-permute-start | bytes 36872 | tf_op jit(solution)/shard_map/ppermute | solution.py:18
  10.1 0.7 copy-start.5
  28.0 1.0 copy-start
  33.8 0.7 copy-start.63
  34.0 8.2 %copy-start.6 = (f32[8,128]{1,0:T(8,128)}, f32[8,128]{1,0:T(8,128)S(1)}, u32[]{:S(2)}) copy-start(f32[8,128]{1,0:T(8,128)S(1)} %get-tuple-element.256) | copy-start | bytes 12292
  34.0 8.2 %copy-start.8 = (f32[8,128]{1,0:T(8,128)}, f32[8,128]{1,0:T(8,128)S(1)}, u32[]{:S(2)}) copy-start(f32[8,128]{1,0:T(8,128)S(1)} %get-tuple-element.259) | copy-start | bytes 12292
  34.0 8.2 %copy-start.10 = (f32[8,128]{1,0:T(8,128)}, f32[8,128]{1,0:T(8,128)S(1)}, u32[]{:S(2)}) copy-start(f32[8,128]{1,0:T(8,128)S(1)} %get-tuple-element.262) | copy-start | bytes 12292
  34.0 8.2 %copy-start.12 = (f32[8,128]{1,0:T(8,128)}, f32[8,128]{1,0:T(8,128)S(1)}, u32[]{:S(2)}) copy-start(f32[8,128]{1,0:T(8,128)S(1)} %get-tuple-element.265) | copy-start | bytes 12292
  34.0 8.2 %copy-start.14 = (f32[8,128]{1,0:T(8,128)}, f32[8,128]{1,0:T(8,128)S(1)}, u32[]{:S(2)}) copy-start(f32[8,128]{1,0:T(8,128)S(1)} %get-tuple-element.268) | copy-start | bytes 12292
  34.0 8.2 %copy-start.16 = (f32[8,128]{1,0:T(8,128)}, f32[8,128]{1,0:T(8,128)S(1)}, u32[]{:S(2)}) copy-start(f32[8,128]{1,0:T(8,128)S(1)} %get-tuple-element.271) | copy-start | bytes 12292
  34.1 8.2 %copy-start.18 = (f32[8,128]{1,0:T(8,128)}, f32[8,128]{1,0:T(8,128)S(1)}, u32[]{:S(2)}) copy-start(f32[8,128]{1,0:T(8,128)S(1)} %get-tuple-element.274) | copy-start | bytes 12292
  34.5 8.6 %copy-start.3 = (f32[256,128]{1,0:T(8,128)S(1)}, f32[256,128]{1,0:T(8,128)}, u32[]{:S(2)}) copy-start(f32[256,128]{1,0:T(8,128)} %param.10) | copy-start | bytes 393220
  42.3 0.9 copy-start.1
  42.3 1.0 copy-start.2
  46.1 0.7 copy-start.61
  46.1 0.7 copy-start.62
  54.5 39.9 %all-to-all-start = ((f32[32,16,128]{2,1,0:T(8,128)}), f32[32,16,128]{2,1,0:T(8,128)S(1)}, u32[]{:S(2)}, u32[]{:S(2)}) async-start(f32[32,16,128]{2,1,0:T(8,128)} %maximum_bitcast_fusion), calls=%async_computation | async-start | bytes 524288 | tf_op jit(solution)/shard_map/all_to_all | solution.py:73
  73.5 0.7 copy-start.23
  73.5 0.7 copy-start.24
  73.5 0.7 copy-start.25
  73.5 0.7 copy-start.26
  73.5 0.7 copy-start.27
  73.5 0.7 copy-start.28
  73.5 0.7 copy-start.29
  73.5 0.7 copy-start.30
  73.5 0.7 copy-start.31
  73.5 0.7 copy-start.32
  73.6 0.7 copy-start.33
  73.6 0.7 copy-start.34
  73.6 0.7 copy-start.36
  73.6 0.7 copy-start.38
  73.6 0.7 copy-start.40
  73.6 0.7 copy-start.55
  73.6 0.7 copy-start.56
  73.7 0.7 copy-start.57
  73.7 0.7 copy-start.58
  73.7 0.7 copy-start.59
  73.7 0.7 copy-start.50
  73.7 0.7 copy-start.51
  73.7 0.7 copy-start.52
  73.7 0.7 copy-start.53
  73.7 0.7 copy-start.54
  73.7 0.7 copy-start.46
  73.7 0.7 copy-start.47
  73.8 0.7 copy-start.48
  73.8 0.7 copy-start.49
  73.8 0.7 copy-start.41
  73.8 0.7 copy-start.42
  73.8 0.7 copy-start.43
  73.8 0.7 copy-start.44
  73.8 0.7 copy-start.45
  73.8 0.7 copy-start.22
  73.8 0.7 copy-start.21
  73.8 0.7 copy-start.20
  94.6 8.2 %collective-permute-start.2 = (f32[16,4]{1,0:T(8,128)S(1)}, f32[16,4]{1,0:T(8,128)S(1)}, u32[]{:S(2)}, u32[]{:S(2)}) collective-permute-start(f32[16,4]{1,0:T(8,128)S(1)} %get-tuple-element.689), channel_id=1, source_target_pairs={{0,1},{1,2},{2,3},{3,4},{4,5},{5,6},{6,7},{7,8},{8,9},{9,10},{10,1... | collective-permute-start | bytes 776 | tf_op jit(solution)/shard_map/ppermute | solution.py:17
  98.0 5.4 %collective-permute-start.3 = (f32[16,4]{1,0:T(8,128)S(1)}, f32[16,4]{1,0:T(8,128)S(1)}, u32[]{:S(2)}, u32[]{:S(2)}) collective-permute-start(f32[16,4]{1,0:T(8,128)S(1)} %get-tuple-element.690), channel_id=1, source_target_pairs={{1,0},{2,1},{3,2},{4,3},{5,4},{6,5},{7,6},{8,7},{9,8},{10,9},{11,1... | collective-permute-start | bytes 776 | tf_op jit(solution)/shard_map/ppermute | solution.py:18
  103.5 0.7 copy-start.19
  103.7 0.7 copy-start.11
  103.7 0.7 copy-start.9
  103.7 0.7 copy-start.7
  104.7 28.8 %copy-start.60 = (f32[8,128]{1,0:T(8,128)}, f32[8,128]{1,0:T(8,128)S(1)}, u32[]{:S(2)}) copy-start(f32[8,128]{1,0:T(8,128)S(1)} %get-tuple-element.5) | copy-start | bytes 12292
  111.2 22.2 %all-to-all-start.1 = ((f32[32,8,128]{2,1,0:T(8,128)}), f32[32,8,128]{2,1,0:T(8,128)S(1)}, u32[]{:S(2)}, u32[]{:S(2)}) async-start(f32[32,8,128]{2,1,0:T(8,128)} %bitcast.609), calls=%async_computation.1 | async-start | bytes 262144 | tf_op jit(solution)/shard_map/all_to_all | solution.py:73
  (6 other events, 4.1 us)

commit v2 on v1

--- a/solution.py
+++ b/solution.py
@@ -1,7 +1,13 @@
+import functools
+
 import jax
 import jax.numpy as jnp
 from jax import lax
+from jax.experimental import pallas as pl
+from jax.experimental.pallas import tpu as pltpu
 from jax.sharding import PartitionSpec as P
+
+MESH = pl.DeviceIdType.MESH
 
 SWEEPS = 4
 STEPS = 2
@@ -62,7 +68,36 @@
     return estimate
 
 
-def reduce_rows(slab, window, step):
+def exchange_kernel(count, chunks_ref, out_ref, recv, send_sem, recv_sem):
+    me = lax.axis_index("long")
+    column = lax.axis_index("aq")
+    barrier = pltpu.get_barrier_semaphore()
+    for k in range(1, count):
+        pl.semaphore_signal(
+            barrier, inc=1, device_id=(lax.rem(me + k, count), column), device_id_type=MESH
+        )
+    pl.semaphore_wait(barrier, count - 1)
+    copies = []
+    for k in range(1, count):
+        peer = lax.rem(me + k, count)
+        copy = pltpu.make_async_remote_copy(
+            src_ref=chunks_ref.at[peer],
+            dst_ref=recv.at[k],
+            send_sem=send_sem.at[k],
+            recv_sem=recv_sem.at[k],
+            device_id=(peer, column),
+            device_id_type=MESH,
+        )
+        copy.start()
+        copies.append(copy)
+    total = chunks_ref[me]
+    for k in range(1, count):
+        copies[k - 1].wait()
+        total = total + recv[k]
+    out_ref[...] = total
+
+
+def reduce_rows(slab, window, step, collective_id):
     count = lax.axis_size("long")
     rows, cols = slab.shape
     edge = (window - step) // 2
@@ -70,8 +105,18 @@
     blocks = padded.reshape(-1, step, cols)
     parts = [blocks[k: k + count] for k in range(window // step)]
     chunks = jnp.stack(parts, axis=1).reshape(count, window, cols)
-    got = lax.all_to_all(chunks, "long", 0, 0, tiled=True)
-    return jnp.sum(got, axis=0)
+    return pl.pallas_call(
+        functools.partial(exchange_kernel, count),
+        out_shape=jax.ShapeDtypeStruct((window, cols), jnp.float32),
+        in_specs=[pl.BlockSpec(memory_space=pltpu.VMEM)],
+        out_specs=pl.BlockSpec(memory_space=pltpu.VMEM),
+        scratch_shapes=[
+            pltpu.VMEM((count, window, cols), jnp.float32),
+            pltpu.SemaphoreType.DMA((count,)),
+            pltpu.SemaphoreType.DMA((count,)),
+        ],
+        compiler_params=pltpu.CompilerParams(collective_id=collective_id, has_side_effects=True),
+    )(chunks)
 
 
 def shards(
@@ -135,7 +180,7 @@
     forcing = column_seed[0] + coupling * heat_1
     forcing = jnp.concatenate([forcing[:-1], (forcing[-1] + gain * recharge_1)[None]], 0)
     water_1 = column_solve(water_faces, forcing)
-    head_1_win = recharge_1_win + reduce_rows(well_slab(water_1[-1]), window, local_rows)
+    head_1_win = recharge_1_win + reduce_rows(well_slab(water_1[-1]), window, local_rows, 0)
 
     heat_2 = column_solve(heat_faces, heat_1)
     head_1_ext = aq_halo(head_1_win, HALO)
@@ -144,7 +189,7 @@
     forcing = water_1 + coupling * heat_2
     forcing = jnp.concatenate([forcing[:-1], (forcing[-1] + gain * recharge_2)[None]], 0)
     water_2 = column_solve(water_faces, forcing)
-    head_2 = recharge_2 + reduce_rows(well_slab(water_2[-1]), local_rows, local_rows)
+    head_2 = recharge_2 + reduce_rows(well_slab(water_2[-1]), local_rows, local_rows, 1)
     return (jnp.stack([water_2, heat_2]), recharge_2, head_2)
 
 

time: 135 us -> 129 us (0.956)
  the two profiles are of different devices: /device:TPU:5 before, /device:TPU:99 now
where the time goes in v2:
time: 129 us; the launch traced here: 128 us
  Pallas kernels  51.6 us (40%)
  other arithmetic  48.7 us (38%)
  starting transfers between devices  14.7 us (11%)
  local copies, waits for them, and re-layouts  6.48 us (5%)
  waiting for transfers between devices  4.12 us (3%)
  between operations  2.84 us (2%)
    pallas_call x2, Pallas kernels, reduce_rows(): pl.pallas_call(functools.partial(exchange_kernel, count), out_shape=jax.S...  51.6 us
    select_n x2, other arithmetic, lookup(): values = jnp.where(texture == number, table_row[number], values)  15.8 us
    scatter-add x2, other arithmetic, well_slab(): owner_slab = jnp.zeros((total_rows * local_cols,), jnp.float32).at[flat_w...  12.5 us
    ppermute x2, starting transfers between devices, aq_halo(): low = lax.ppermute(block[..., block.shape[-1] - width:], 'aq', forward)  9.41 us
    add x1, other arithmetic, shards(): forcing = column_seed[0] + coupling * heat_1  7.93 us
    ppermute x2, starting transfers between devices, aq_halo(): high = lax.ppermute(block[..., :width], 'aq', backward)  5.28 us
    unnamed x173, local copies, waits for them, and re-layouts  4.68 us
    ppermute x2, waiting for transfers between devices, aq_halo(): high = lax.ppermute(block[..., :width], 'aq', backward)  4.12 us
  transfers between devices with their start and end apart: 4, of which 1 were waited for; matrix products, arithmetic and copies ran while one was open for 23% of the time, Pallas kernels for 0%

profile of v2, /device:TPU:99, one launch (start us, length us, event | category | flops | bytes accessed | tf_op | source)
XLA Modules:
  0.0 128.4 jit_solution(1513781981021387456)
XLA Ops:
  0.6 1.1 pad_maximum_fusion.1
  1.7 0.0 copy-start.4
  1.7 0.2 fusion.1056
  1.9 1.9 %collective-permute-start = (f32[3,256,4]{2,1,0:T(8,128)S(1)}, f32[3,256,4]{2,1,0:T(8,128)S(1)}, u32[]{:S(2)}, u32[]{:S(2)}) collective-permute-start(f32[3,256,4]{2,1,0:T(8,128)S(1)} %get-tuple-element.679), channel_id=1, source_target_pairs={{0,1},{1,2},{2,3},{3,4},{4,5},{5,6},{6,7},{7,8},{8,9},{9,10},{10,1... | collective-permute-start | bytes 36872 | tf_op jit(solution)/shard_map/ppermute | solution.py:23
  3.8 3.4 %collective-permute-start.1 = (f32[3,256,4]{2,1,0:T(8,128)S(1)}, f32[3,256,4]{2,1,0:T(8,128)}, u32[]{:S(2)}, u32[]{:S(2)}) collective-permute-start(f32[3,256,4]{2,1,0:T(8,128)S(1)} %get-tuple-element.680), channel_id=1, source_target_pairs={{1,0},{2,1},{3,2},{4,3},{5,4},{6,5},{7,6},{8,7},{9,8},{10,9},{11,1... | collective-permute-start | bytes 36872 | tf_op jit(solution)/shard_map/ppermute | solution.py:24
  7.2 0.0 copy-start.5
  7.2 0.6 copy-done.5
  7.9 0.7 fusion.1058
  8.6 0.7 fusion.1059
  9.3 7.9 %select_select_fusion = (f32[64,8,128]{2,1,0:T(8,128)S(1)}, pred[64,8,128]{2,1,0:T(8,128)(4,1)S(1)}, pred[64,8,128]{2,1,0:T(8,128)(4,1)S(1)}, pred[64,8,128]{2,1...) fusion(f32[]{:T(128)} %bitcast.250, ...), kind=kLoop, calls=%fused_computation.312 | loop fusion | flops 1572864 | bytes 1310768 | tf_op jit(solution)/shard_map/jit(_where)/select_n | solution.py:31
  17.3 7.8 %select_select_fusion.1 = f32[64,8,128]{2,1,0:T(8,128)S(1)} fusion(pred[64,8,128]{2,1,0:T(8,128)(4,1)S(1)} %get-tuple-element.391, pred[64,8,128]{2,1,0:T(8,128)(4,1)S(1)} %get-tuple-element.390, pred[64,8,128]{2,1,0:T(8,128)(4,1)S(1)} %get-tuple-element.389, pred[64,8,128]{2,1,0:T(8,128)(4,1)S(1)} %get-tuple-element.388, ...), kind=kLoop, calls=%fused_computation.313 | loop fusion | flops 786432 | bytes 1048624 | tf_op jit(solution)/shard_map/jit(_where)/select_n | solution.py:31
  25.1 0.0 copy-start
  25.2 0.9 copy-done
  26.2 0.1 fusion.613
  26.2 0.3 fusion.486
  26.6 0.3 fusion.363
  26.9 0.2 fusion.413
  27.1 0.2 constant_dynamic-update-slice_fusion.63
  27.4 0.4 fusion.420
  27.7 0.4 constant_dynamic-update-slice_fusion.191
  28.1 0.5 constant_dynamic-update-slice_fusion.62
  28.6 0.2 add_divide_fusion.11
  28.8 0.6 constant_dynamic-update-slice_fusion.189
  30.8 0.0 copy-start.10
  30.9 0.2 fusion.677
  31.1 0.5 copy-done.10
  31.5 7.9 %bitcast_add_fusion = (f32[64,8,128]{2,1,0:T(8,128)S(1)}, f32[64,8,128]{2,1,0:T(8,128)S(1)}) fusion(f32[64,8,128]{2,1,0:T(8,128)S(1)} %constant_dynamic-update-slice_fusion, f32[2,64,8,128]{3,2,1,0:T(8,128)S(1)} %copy-done, pred[64,8,128]{2,1,0:T(8,128)(4,1)S(1)} %get-tuple-element.391, pred[64,8,128]{2,1,0:T(8,128)(4,1)S(1)} %get-tuple-element.390, ...), kind=kLoop, calls=%fused_computation.310 | loop fusion | flops 983040 | bytes 1835056 | tf_op jit(solution)/shard_map/add | solution.py:180
  39.5 0.0 copy-start.1
  39.5 0.0 copy-start.2
  39.5 0.1 fusion.298
  39.6 0.0 collective-permute-done
  39.7 0.7 copy-done.1
  40.4 0.1 copy-done.2
  40.5 1.4 %select_maximum_fusion = f32[3,264,136]{2,1,0:T(8,128)S(1)} fusion(f32[3,256,4]{2,1,0:T(8,128)} %collective-permute-done.1, f32[3,256,4]{2,1,0:T(8,128)S(1)} %collective-permute-done, f32[1,256,128]{2,1,0:T(8,128)S(1)} %bitcast.7746, f32[1,256,128]{2,1,0:T(8,128)S(1)} %bitcast.7748, f32[1,256,128]{2,1,0:T(8,128)S(1)} %bitcast.7750), kind=kLoop, calls=%fused_computation.4 | loop fusion | flops 1292544 | bytes 848640 | tf_op jit(solution)/shard_map/concatenate | solution.py:25
  41.9 0.6 fusion.8
  42.5 0.3 divide_add_fusion.1
  42.8 0.3 divide_add_fusion
  43.1 0.2 multiply_add_fusion
  43.3 0.0 copy-start.8
  43.3 0.0 copy-start.9
  43.4 0.6 copy-done.8
  44.0 0.0 copy-done.9
  44.0 0.3 multiply_bitcast_fusion.1
  44.4 6.0 %scatter_custom_fusion = f32[32768]{0:T(1024)S(1)} fusion(s32[1024]{0:T(1024)S(1)} %bitcast.7753, f32[1024]{0:T(1024)S(1)} %get-tuple-element.102, f32[]{:T(128)} %constant.39.clone.1), kind=kCustom, calls=%fused_computation.335 | custom fusion | flops 1024 | bytes 131076 | tf_op jit(solution)/shard_map/scatter-add | solution.py:170
  50.4 0.7 maximum_bitcast_fusion.chunks_ref
  51.1 29.7 %shard_map.112 = f32[16,128]{1,0:T(8,128)} custom-call(f32[32,16,128]{2,1,0:T(8,128)} %maximum_bitcast_fusion.chunks_ref), custom_call_target="tpu_custom_call" | custom-call | tf_op jit(solution)/shard_map/pallas_call | solution.py:108
  80.8 0.8 slice_add_fusion.2
  81.6 0.1 fusion.1057
  81.7 7.5 %collective-permute-start.2 = (f32[16,4]{1,0:T(8,128)S(1)}, f32[16,4]{1,0:T(8,128)S(1)}, u32[]{:S(2)}, u32[]{:S(2)}) collective-permute-start(f32[16,4]{1,0:T(8,128)S(1)} %get-tuple-element.689), channel_id=1, source_target_pairs={{0,1},{1,2},{2,3},{3,4},{4,5},{5,6},{6,7},{7,8},{8,9},{9,10},{10,1... | collective-permute-start | bytes 776 | tf_op jit(solution)/shard_map/ppermute | solution.py:23
  89.2 1.9 %collective-permute-start.3 = (f32[16,4]{1,0:T(8,128)S(1)}, f32[16,4]{1,0:T(8,128)S(1)}, u32[]{:S(2)}, u32[]{:S(2)}) collective-permute-start(f32[16,4]{1,0:T(8,128)S(1)} %get-tuple-element.690), channel_id=1, source_target_pairs={{1,0},{2,1},{3,2},{4,3},{5,4},{6,5},{7,6},{8,7},{9,8},{10,9},{11,1... | collective-permute-start | bytes 776 | tf_op jit(solution)/shard_map/ppermute | solution.py:24
  91.1 0.2 constant_dynamic-update-slice_fusion.127
  92.1 0.1 multiply_add_fusion.1
  92.1 4.1 %collective-permute-done.3 = f32[16,4]{1,0:T(8,128)S(1)} collective-permute-done((f32[16,4]{1,0:T(8,128)S(1)}, f32[16,4]{1,0:T(8,128)S(1)}, u32[]{:S(2)}, u32[]{:S(2)}) %collective-permute-start.3) | collective-permute-done | bytes 288 | tf_op jit(solution)/shard_map/ppermute | solution.py:24
  96.2 0.1 fusion.66
  96.3 0.1 fusion.37
  96.4 0.1 fusion.49
  96.5 0.1 fusion.55
  96.6 0.3 multiply_bitcast_fusion
  96.9 6.5 %scatter_custom_fusion.1 = f32[32768]{0:T(1024)} fusion(s32[1024]{0:T(1024)S(1)} %bitcast.7754, f32[1024]{0:T(1024)S(1)} %get-tuple-element.3, f32[]{:T(128)} %constant.39.clone.1), kind=kCustom, calls=%fused_computation.333 | custom fusion | flops 1024 | bytes 131076 | tf_op jit(solution)/shard_map/scatter-add | solution.py:170
  103.4 21.9 %shard_map.113 = f32[8,128]{1,0:T(8,128)} custom-call(f32[32,8,128]{2,1,0:T(8,128)} %bitcast.7744), custom_call_target="tpu_custom_call" | custom-call | tf_op jit(solution)/shard_map/pallas_call | solution.py:108
  125.3 0.2 constant_dynamic-update-slice_fusion.255
  126.3 0.7 copy-done.7
  127.0 0.6 add.22522
  127.6 0.8 pad_maximum_fusion
  (270 shorter events, 1.4 us)
Async XLA Ops:
  1.7 7.6 %copy-start.4 = (s32[64,8,128]{2,1,0:T(8,128)S(1)}, s32[64,8,128]{2,1,0:T(8,128)}, u32[]{:S(2)}) copy-start(s32[64,8,128]{2,1,0:T(8,128)} %param.11) | copy-start | bytes 786436
  1.9 37.8 %collective-permute-start = (f32[3,256,4]{2,1,0:T(8,128)S(1)}, f32[3,256,4]{2,1,0:T(8,128)S(1)}, u32[]{:S(2)}, u32[]{:S(2)}) collective-permute-start(f32[3,256,4]{2,1,0:T(8,128)S(1)} %get-tuple-element.679), channel_id=1, source_target_pairs={{0,1},{1,2},{2,3},{3,4},{4,5},{5,6},{6,7},{7,8},{8,9},{9,10},{10,1... | collective-permute-start | bytes 36872 | tf_op jit(solution)/shard_map/ppermute | solution.py:23
  3.8 35.8 %collective-permute-start.1 = (f32[3,256,4]{2,1,0:T(8,128)S(1)}, f32[3,256,4]{2,1,0:T(8,128)}, u32[]{:S(2)}, u32[]{:S(2)}) collective-permute-start(f32[3,256,4]{2,1,0:T(8,128)S(1)} %get-tuple-element.680), channel_id=1, source_target_pairs={{1,0},{2,1},{3,2},{4,3},{5,4},{6,5},{7,6},{8,7},{9,8},{10,9},{11,1... | collective-permute-start | bytes 36872 | tf_op jit(solution)/shard_map/ppermute | solution.py:24
  7.2 0.7 copy-start.5
  25.1 1.0 copy-start
  30.8 0.7 copy-start.10
  31.5 8.1 %copy-start.3 = (f32[256,128]{1,0:T(8,128)S(1)}, f32[256,128]{1,0:T(8,128)}, u32[]{:S(2)}) copy-start(f32[256,128]{1,0:T(8,128)} %param.10) | copy-start | bytes 393220
  39.5 0.9 copy-start.1
  39.5 1.0 copy-start.2
  43.3 0.7 copy-start.8
  43.3 0.7 copy-start.9
  81.7 10.5 %collective-permute-start.2 = (f32[16,4]{1,0:T(8,128)S(1)}, f32[16,4]{1,0:T(8,128)S(1)}, u32[]{:S(2)}, u32[]{:S(2)}) collective-permute-start(f32[16,4]{1,0:T(8,128)S(1)} %get-tuple-element.689), channel_id=1, source_target_pairs={{0,1},{1,2},{2,3},{3,4},{4,5},{5,6},{6,7},{7,8},{8,9},{9,10},{10,1... | collective-permute-start | bytes 776 | tf_op jit(solution)/shard_map/ppermute | solution.py:23
  89.2 7.1 %collective-permute-start.3 = (f32[16,4]{1,0:T(8,128)S(1)}, f32[16,4]{1,0:T(8,128)S(1)}, u32[]{:S(2)}, u32[]{:S(2)}) collective-permute-start(f32[16,4]{1,0:T(8,128)S(1)} %get-tuple-element.690), channel_id=1, source_target_pairs={{1,0},{2,1},{3,2},{4,3},{5,4},{6,5},{7,6},{8,7},{9,8},{10,9},{11,1... | collective-permute-start | bytes 776 | tf_op jit(solution)/shard_map/ppermute | solution.py:24
  96.9 29.4 %copy-start.6 = (f32[8,128]{1,0:T(8,128)}, f32[8,128]{1,0:T(8,128)S(1)}, u32[]{:S(2)}) copy-start(f32[8,128]{1,0:T(8,128)S(1)} %get-tuple-element.5) | copy-start | bytes 12292
  126.3 0.7 copy-start.7

commit v3 on v2

--- a/solution.py
+++ b/solution.py
@@ -25,36 +25,94 @@
     return jnp.concatenate([low, block, high], axis=-1)
 
 
-def lookup(texture, table_row):
-    values = jnp.zeros(texture.shape, jnp.float32)
-    for number in range(table_row.shape[0]):
-        values = jnp.where(texture == number, table_row[number], values)
-    return values
-
-
-def column_solve(faces, forcing):
-    layer_count = forcing.shape[0]
-    ratios = []
-    partials = []
-    for layer_index in range(layer_count):
-        diagonal = jnp.ones_like(forcing[0])
-        if layer_index > 0:
-            diagonal = diagonal + faces[layer_index - 1]
-        if layer_index < layer_count - 1:
-            diagonal = diagonal + faces[layer_index]
-        if layer_index == 0:
-            pivot_value = diagonal
-            carried = forcing[0]
-        else:
-            pivot_value = diagonal - faces[layer_index - 1] * ratios[-1]
-            carried = forcing[layer_index] + faces[layer_index - 1] * partials[-1]
-        if layer_index < layer_count - 1:
-            ratios.append(faces[layer_index] / pivot_value)
-        partials.append(carried / pivot_value)
-    solution = [partials[-1]]
-    for layer_index in range(layer_count - 2, -1, -1):
-        solution.append(partials[layer_index] + ratios[layer_index] * solution[-1])
-    return jnp.stack(solution[::-1])
+def column_kernel(
+    table, tex, seed, heat_1, heat_2, c_out, d_out, b_out, a_last,
+    wnum, hnum, coup, wface, hface, wratio, wpivot, hratio, hpivot, part_a, part_b, part_c, a_sol,
+):
+    layers = tex.shape[0]
+    classes = table.shape[1]
+    for l in range(layers):
+        t = tex[l]
+        w = jnp.zeros(t.shape, jnp.float32)
+        h = jnp.zeros(t.shape, jnp.float32)
+        c = jnp.zeros(t.shape, jnp.float32)
+        for k in range(classes):
+            m = t == k
+            w = jnp.where(m, table[0, k], w)
+            h = jnp.where(m, table[1, k], h)
+            c = jnp.where(m, table[2, k], c)
+        wnum[l] = w
+        hnum[l] = h
+        coup[l] = 0.2 * c
+    for l in range(layers - 1):
+        wface[l] = 0.5 * (wnum[l] + wnum[l + 1])
+        hface[l] = 0.5 * (hnum[l] + hnum[l + 1])
+
+    def factor(l, face, ratio, pivot, prev):
+        diagonal = jnp.ones(tex.shape[1:], jnp.float32)
+        if l > 0:
+            diagonal = diagonal + face[l - 1]
+        if l < layers - 1:
+            diagonal = diagonal + face[l]
+        p = diagonal if l == 0 else diagonal - face[l - 1] * prev
+        pivot[l] = p
+        if l < layers - 1:
+            r = face[l] / p
+            ratio[l] = r
+            return r
+        return None
+
+    def forward(l, face, pivot, forcing, part, prev):
+        carried = forcing if l == 0 else forcing + face[l - 1] * prev
+        value = carried / pivot[l]
+        part[l] = value
+        return value
+
+    def backward(l, ratio, part, out, prev):
+        value = part[l] if l == layers - 1 else part[l] + ratio[l] * prev
+        out[l] = value
+        return value
+
+    wr = hr = hp = None
+    for l in range(layers):
+        wr = factor(l, wface, wratio, wpivot, wr)
+        hr = factor(l, hface, hratio, hpivot, hr)
+        hp = forward(l, hface, hpivot, seed[1, l], part_a, hp)
+    h1 = b = None
+    for l in range(layers - 1, -1, -1):
+        h1 = backward(l, hratio, part_a, heat_1, h1)
+        b = 1.0 / wpivot[l] if l == layers - 1 else wratio[l] * b
+        b_out[l] = b
+    hp = ap = dp = None
+    for l in range(layers):
+        hp = forward(l, hface, hpivot, heat_1[l], part_a, hp)
+        ap = forward(l, wface, wpivot, seed[0, l] + coup[l] * heat_1[l], part_b, ap)
+        dp = forward(l, wface, wpivot, b_out[l], part_c, dp)
+    a_last[...] = ap
+    h2 = a = d = None
+    for l in range(layers - 1, -1, -1):
+        h2 = backward(l, hratio, part_a, heat_2, h2)
+        a = backward(l, wratio, part_b, a_sol, a)
+        d = backward(l, wratio, part_c, d_out, d)
+    cp = None
+    for l in range(layers):
+        cp = forward(l, wface, wpivot, a_sol[l] + coup[l] * heat_2[l], part_b, cp)
+    c = None
+    for l in range(layers - 1, -1, -1):
+        c = backward(l, wratio, part_b, c_out, c)
+
+
+def column_solves(soil_table, texture, column_seed):
+    layers, rows, cols = texture.shape
+    full = jax.ShapeDtypeStruct((layers, rows, cols), jnp.float32)
+    vmem = pl.BlockSpec(memory_space=pltpu.VMEM)
+    return pl.pallas_call(
+        column_kernel,
+        out_shape=(full, full, full, full, full, jax.ShapeDtypeStruct((rows, cols), jnp.float32)),
+        in_specs=[pl.BlockSpec(memory_space=pltpu.SMEM), vmem, vmem],
+        out_specs=(vmem,) * 6,
+        scratch_shapes=[pltpu.VMEM((layers, rows, cols), jnp.float32)] * 13,
+    )(soil_table, texture, column_seed)
 
 
 def relax(forcing_head, face_set, diagonal):
@@ -97,14 +155,17 @@
     out_ref[...] = total
 
 
-def reduce_rows(slab, window, step, collective_id):
+def reduce_rows(term, wells, window, step, collective_id):
     count = lax.axis_size("long")
-    rows, cols = slab.shape
+    cols = term.shape[1]
     edge = (window - step) // 2
-    padded = jnp.pad(slab, ((edge, edge), (0, 0)))
-    blocks = padded.reshape(-1, step, cols)
-    parts = [blocks[k: k + count] for k in range(window // step)]
-    chunks = jnp.stack(parts, axis=1).reshape(count, window, cols)
+    flat_wells = wells.reshape(1, -1)
+    slot = lax.broadcasted_iota(jnp.int32, (count * window, 1), 0)
+    target_row = (slot // window) * step - edge + slot % window
+    spread = jnp.where(flat_wells // cols == target_row, term.reshape(1, -1), 0.0)
+    picks = flat_wells.reshape(-1, 1) % cols == lax.broadcasted_iota(jnp.int32, (1, cols), 1)
+    chunks = jnp.dot(spread, picks.astype(jnp.float32), precision=lax.Precision.HIGHEST)
+    chunks = chunks.reshape(count, window, cols)
     return pl.pallas_call(
         functools.partial(exchange_kernel, count),
         out_shape=jax.ShapeDtypeStruct((window, cols), jnp.float32),
@@ -128,11 +189,7 @@
     total_cols = local_cols * lax.axis_size("aq")
     row_start = lax.axis_index("long") * local_rows
     col_start = lax.axis_index("aq") * local_cols
-    water_number = lookup(texture, soil_table[0])
-    heat_number = lookup(texture, soil_table[1])
-    coupling = 0.2 * lookup(texture, soil_table[2])
-    water_faces = 0.5 * (water_number[:-1] + water_number[1:])
-    heat_faces = 0.5 * (heat_number[:-1] + heat_number[1:])
+    heat_1, heat_2, c_sol, d_sol, b_sol, a_last = column_solves(soil_table, texture, column_seed)
     gain = jnp.where(active == 1, conductance, 0.0)
 
     fields = aq_halo(jnp.stack([head_seed, transmissivity, storage]), HALO)
@@ -159,37 +216,22 @@
 
     face_win = tuple(window_of(f) for f in face_set)
     diag_win = window_of(diagonal)
-
-    flat_wells = wells.reshape(-1)
-
-    def well_slab(water_bottom):
-        well_term = gain * water_bottom
-        owner_slab = (
-            jnp.zeros((total_rows * local_cols,), jnp.float32)
-            .at[flat_wells]
-            .add(well_term.reshape(-1))
-        )
-        return owner_slab.reshape(total_rows, local_cols)
-
     core = slice(HALO, HALO + local_rows), slice(HALO, HALO + local_cols)
 
-    heat_1 = column_solve(heat_faces, column_seed[1])
     estimate_1 = relax(head_ext, face_set, diagonal)
     recharge_1_win = window_of(estimate_1)[:, HALO:HALO + local_cols]
     recharge_1 = recharge_1_win[HALO:HALO + local_rows]
-    forcing = column_seed[0] + coupling * heat_1
-    forcing = jnp.concatenate([forcing[:-1], (forcing[-1] + gain * recharge_1)[None]], 0)
-    water_1 = column_solve(water_faces, forcing)
-    head_1_win = recharge_1_win + reduce_rows(well_slab(water_1[-1]), window, local_rows, 0)
-
-    heat_2 = column_solve(heat_faces, heat_1)
+    r_1 = gain * recharge_1
+    term_1 = gain * (a_last + r_1 * b_sol[-1])
+    head_1_win = recharge_1_win + reduce_rows(term_1, wells, window, local_rows, 0)
+
     head_1_ext = aq_halo(head_1_win, HALO)
     estimate_2 = relax(head_1_ext, face_win, diag_win)
     recharge_2 = estimate_2[core]
-    forcing = water_1 + coupling * heat_2
-    forcing = jnp.concatenate([forcing[:-1], (forcing[-1] + gain * recharge_2)[None]], 0)
-    water_2 = column_solve(water_faces, forcing)
-    head_2 = recharge_2 + reduce_rows(well_slab(water_2[-1]), local_rows, local_rows, 1)
+    r_2 = gain * recharge_2
+    term_2 = gain * (c_sol[-1] + r_1 * d_sol[-1] + r_2 * b_sol[-1])
+    head_2 = recharge_2 + reduce_rows(term_2, wells, local_rows, local_rows, 1)
+    water_2 = c_sol + r_1 * d_sol + r_2 * b_sol
     return (jnp.stack([water_2, heat_2]), recharge_2, head_2)
 
 

time: 129 us -> 99.6 us (0.77)
  the two profiles are of different devices: /device:TPU:99 before, /device:TPU:5 now
where the time goes in v3:
time: 99.6 us; the launch traced here: 99.2 us
  Pallas kernels  58.2 us (58%)
  starting transfers between devices  16.2 us (16%)
  waiting for transfers between devices  13 us (13%)
  other arithmetic  5.64 us (6%)
  matrix products  3.46 us (3%)
  local copies, waits for them, and re-layouts  1.63 us (2%)
    pallas_call x2, Pallas kernels, reduce_rows(): pl.pallas_call(functools.partial(exchange_kernel, count), out_shape=jax.S...  54.6 us
    ppermute x2, starting transfers between devices, aq_halo(): high = lax.ppermute(block[..., :width], 'aq', backward)  10.6 us
    ppermute x2, waiting for transfers between devices, aq_halo(): high = lax.ppermute(block[..., :width], 'aq', backward)  10 us
    ppermute x2, starting transfers between devices, aq_halo(): low = lax.ppermute(block[..., block.shape[-1] - width:], 'aq', forward)  5.65 us
    pallas_call x1, Pallas kernels, column_solves(): pl.pallas_call(column_kernel, out_shape=(full, full, full, full, full, ja...  3.69 us
    dot_general x2, matrix products, reduce_rows(): jnp.dot(spread, picks.astype(jnp.float32), precision=lax.Precision.HIGHEST)  3.46 us
    ppermute x2, waiting for transfers between devices, aq_halo(): low = lax.ppermute(block[..., block.shape[-1] - width:], 'aq', forward)  3.01 us
  transfers between devices with their start and end apart: 4, of which 3 were waited for; matrix products, arithmetic and copies ran while one was open for 0% of the time, Pallas kernels for 4%

profile of v3, /device:TPU:5, one launch (start us, length us, event | category | flops | bytes accessed | tf_op | source)
XLA Modules:
  0.0 99.2 jit_solution(2030797383411754324)
XLA Ops:
  0.6 1.1 %pad_maximum_fusion.1 = f32[3,256,128]{2,1,0:T(8,128)S(1)} fusion(f32[1,256,128]{2,1,0:T(8,128)} %bitcast.85, f32[1,256,128]{2,1,0:T(8,128)} %bitcast.87, f32[1,256,128]{2,1,0:T(8,128)} %bitcast.89), kind=kLoop, calls=%fused_computation.27 | loop fusion | flops 196608 | bytes 786432 | tf_op jit(solution)/shard_map/stack | solution.py:195
  1.7 0.0 copy-start.9
  1.7 0.2 fusion.122
  1.9 0.0 copy-start
  1.9 0.0 copy-start.1
  1.9 0.0 copy-start.2
  1.9 3.7 %collective-permute-start = (f32[3,256,4]{2,1,0:T(8,128)S(1)}, f32[3,256,4]{2,1,0:T(8,128)S(1)}, u32[]{:S(2)}, u32[]{:S(2)}) collective-permute-start(f32[3,256,4]{2,1,0:T(8,128)S(1)} %get-tuple-element.29), channel_id=1, source_target_pairs={{0,1},{1,2},{2,3},{3,4},{4,5},{5,6},{6,7},{7,8},{8,9},{9,10},{10,1... | collective-permute-start | bytes 36872 | tf_op jit(solution)/shard_map/ppermute | solution.py:23
  5.6 4.6 %collective-permute-start.1 = (f32[3,256,4]{2,1,0:T(8,128)S(1)}, f32[3,256,4]{2,1,0:T(8,128)S(1)}, u32[]{:S(2)}, u32[]{:S(2)}) collective-permute-start(f32[3,256,4]{2,1,0:T(8,128)S(1)} %get-tuple-element.30), channel_id=1, source_target_pairs={{1,0},{2,1},{3,2},{4,3},{5,4},{6,5},{7,6},{8,7},{9,8},{10,9},{11,1... | collective-permute-start | bytes 36872 | tf_op jit(solution)/shard_map/ppermute | solution.py:24
  10.3 0.0 copy-done.9
  10.3 3.7 %shard_map.112 = (f32[64,8,128]{2,1,0:T(8,128)}, f32[64,8,128]{2,1,0:T(8,128)}, f32[64,8,128]{2,1,0:T(8,128)}, f32[64,8,128]{2,1,0:T(8,128)}, f32[64,8,128]{2,1,0:T(8,128)}, /*index=5*/f32[8,128]{1,0:T(8,128)}) custom-call(f32[3,12]{1,0:T(4,128)} %table.1, s32[64,8,128]{2,1,0:T(8,128)} %tex.1, f32[2,64,8,128]{3,2,1,0:T(8,128)} %seed.1), custom_call_target="tpu_custom_call" | custom-call | tf_op jit(solution)/shard_map/pallas_call | solution.py:109
  14.0 3.0 %collective-permute-done = f32[3,256,4]{2,1,0:T(8,128)S(1)} collective-permute-done((f32[3,256,4]{2,1,0:T(8,128)S(1)}, f32[3,256,4]{2,1,0:T(8,128)S(1)}, u32[]{:S(2)}, u32[]{:S(2)}) %collective-permute-start) | collective-permute-done | bytes 12320 | tf_op jit(solution)/shard_map/ppermute | solution.py:23
  17.0 9.3 %collective-permute-done.1 = f32[3,256,4]{2,1,0:T(8,128)S(1)} collective-permute-done((f32[3,256,4]{2,1,0:T(8,128)S(1)}, f32[3,256,4]{2,1,0:T(8,128)S(1)}, u32[]{:S(2)}, u32[]{:S(2)}) %collective-permute-start.1) | collective-permute-done | bytes 12320 | tf_op jit(solution)/shard_map/ppermute | solution.py:24
  26.3 0.0 copy-done
  26.3 0.0 copy-done.1
  26.3 0.0 copy-done.2
  26.3 0.4 select_maximum_fusion
  26.8 0.6 fusion.21
  27.3 0.3 divide_add_fusion.1
  27.6 0.3 divide_add_fusion
  27.9 0.0 copy-start.3
  27.9 0.0 copy-start.10
  27.9 0.0 copy-start.11
  28.0 0.0 copy-start.12
  28.0 0.2 multiply_add_fusion
  28.2 0.7 copy-done.3
  28.9 0.0 copy-done.10
  28.9 0.0 copy-done.11
  28.9 0.0 copy-done.12
  28.9 0.1 fusion.93
  29.0 2.0 %fusion = f32[512,128]{1,0:T(8,128)} fusion(f32[1024]{0:T(1024)S(1)} %get-tuple-element.18, s32[1024]{0:T(1024)S(1)} %get-tuple-element.38, s32[512]{0:T(512)S(1)} %fusion.103, s32[1024]{0:T(1024)S(1)} %get-tuple-element.37), kind=kOutput, calls=%fused_computation | convolution fusion | flops 806486016 | bytes 276480 | tf_op jit(solution)/shard_map/dot_general | solution.py:167
  31.0 0.0 copy-start.4
  31.0 0.0 copy-start.5
  31.0 33.5 %shard_map.113 = f32[16,128]{1,0:T(8,128)} custom-call(f32[32,16,128]{2,1,0:T(8,128)} %bitcast.91), custom_call_target="tpu_custom_call" | custom-call | tf_op jit(solution)/shard_map/pallas_call | solution.py:169
  64.5 0.8 slice_add_fusion
  65.2 0.1 fusion.123
  65.3 2.0 %collective-permute-start.2 = (f32[16,4]{1,0:T(8,128)S(1)}, f32[16,4]{1,0:T(8,128)S(1)}, u32[]{:S(2)}, u32[]{:S(2)}) collective-permute-start(f32[16,4]{1,0:T(8,128)S(1)} %get-tuple-element.35), channel_id=1, source_target_pairs={{0,1},{1,2},{2,3},{3,4},{4,5},{5,6},{6,7},{7,8},{8,9},{9,10},{10,1... | collective-permute-start | bytes 776 | tf_op jit(solution)/shard_map/ppermute | solution.py:23
  67.3 6.0 %collective-permute-start.3 = (f32[16,4]{1,0:T(8,128)S(1)}, f32[16,4]{1,0:T(8,128)S(1)}, u32[]{:S(2)}, u32[]{:S(2)}) collective-permute-start(f32[16,4]{1,0:T(8,128)S(1)} %get-tuple-element.36), channel_id=1, source_target_pairs={{1,0},{2,1},{3,2},{4,3},{5,4},{6,5},{7,6},{8,7},{9,8},{10,9},{11,1... | collective-permute-start | bytes 776 | tf_op jit(solution)/shard_map/ppermute | solution.py:24
  73.3 0.0 collective-permute-done.2
  73.3 0.7 collective-permute-done.3
  74.1 0.1 fusion.75
  74.2 0.1 fusion.46
  74.3 0.1 fusion.58
  74.4 0.1 fusion.64
  74.4 0.0 copy-done.4
  74.4 0.0 copy-done.5
  74.4 0.1 fusion.90
  74.5 0.0 copy-start.8
  74.5 1.5 %convolution_bitcast_fusion.chunks_ref = f32[32,8,128]{2,1,0:T(8,128)} fusion(f32[1024]{0:T(1024)S(1)} %get-tuple-element.13, s32[1024]{0:T(1024)S(1)} %get-tuple-element.38, s32[256]{0:T(256)S(1)} %fusion.113, s32[1024]{0:T(1024)S(1)} %get-tuple-element.37), kind=kOutput, calls=%fused_computation.5 | convolution fusion | flops 403308544 | bytes 144384 | tf_op jit(solution)/shard_map/dot_general | solution.py:167
  76.0 0.0 copy-start.6
  76.0 21.1 %shard_map.114 = f32[8,128]{1,0:T(8,128)} custom-call(f32[32,8,128]{2,1,0:T(8,128)} %convolution_bitcast_fusion.chunks_ref), custom_call_target="tpu_custom_call" | custom-call | tf_op jit(solution)/shard_map/pallas_call | solution.py:169
  97.1 0.0 copy-start.7
  97.1 0.0 copy-done.8
  97.1 0.6 copy-done.7
  97.7 0.6 add.315
  98.3 0.0 copy-done.6
  98.3 0.8 pad_maximum_fusion
  (12 shorter events, 0.2 us)
Async XLA Ops:
  1.7 8.6 %copy-start.9 = (s32[8,128]{1,0:T(8,128)S(1)}, s32[8,128]{1,0:T(8,128)}, u32[]{:S(2)}) copy-start(s32[8,128]{1,0:T(8,128)} %param.15) | copy-start | bytes 12292
  1.9 24.4 %copy-start = (f32[256,128]{1,0:T(8,128)S(1)}, f32[256,128]{1,0:T(8,128)}, u32[]{:S(2)}) copy-start(f32[256,128]{1,0:T(8,128)} %param.17) | copy-start | bytes 393220
  1.9 24.4 %copy-start.1 = (f32[256,128]{1,0:T(8,128)S(1)}, f32[256,128]{1,0:T(8,128)}, u32[]{:S(2)}) copy-start(f32[256,128]{1,0:T(8,128)} %param.16) | copy-start | bytes 393220
  1.9 24.4 %copy-start.2 = (f32[256,128]{1,0:T(8,128)S(1)}, f32[256,128]{1,0:T(8,128)}, u32[]{:S(2)}) copy-start(f32[256,128]{1,0:T(8,128)} %param.10) | copy-start | bytes 393220
  1.9 15.1 %collective-permute-start = (f32[3,256,4]{2,1,0:T(8,128)S(1)}, f32[3,256,4]{2,1,0:T(8,128)S(1)}, u32[]{:S(2)}, u32[]{:S(2)}) collective-permute-start(f32[3,256,4]{2,1,0:T(8,128)S(1)} %get-tuple-element.29), channel_id=1, source_target_pairs={{0,1},{1,2},{2,3},{3,4},{4,5},{5,6},{6,7},{7,8},{8,9},{9,10},{10,1... | collective-permute-start | bytes 36872 | tf_op jit(solution)/shard_map/ppermute | solution.py:23
  5.6 20.7 %collective-permute-start.1 = (f32[3,256,4]{2,1,0:T(8,128)S(1)}, f32[3,256,4]{2,1,0:T(8,128)S(1)}, u32[]{:S(2)}, u32[]{:S(2)}) collective-permute-start(f32[3,256,4]{2,1,0:T(8,128)S(1)} %get-tuple-element.30), channel_id=1, source_target_pairs={{1,0},{2,1},{3,2},{4,3},{5,4},{6,5},{7,6},{8,7},{9,8},{10,9},{11,1... | collective-permute-start | bytes 36872 | tf_op jit(solution)/shard_map/ppermute | solution.py:24
  27.9 1.0 copy-start.3
  27.9 0.9 copy-start.10
  27.9 0.9 copy-start.11
  28.0 0.9 copy-start.12
  31.0 43.5 %copy-start.4 = (f32[64,8,128]{2,1,0:T(8,128)S(1)}, f32[64,8,128]{2,1,0:T(8,128)}, u32[]{:S(2)}) copy-start(f32[64,8,128]{2,1,0:T(8,128)} %get-tuple-element.8) | copy-start | bytes 786436
  31.0 43.5 %copy-start.5 = (f32[64,8,128]{2,1,0:T(8,128)S(1)}, f32[64,8,128]{2,1,0:T(8,128)}, u32[]{:S(2)}) copy-start(f32[64,8,128]{2,1,0:T(8,128)} %get-tuple-element.9) | copy-start | bytes 786436
  65.3 8.0 %collective-permute-start.2 = (f32[16,4]{1,0:T(8,128)S(1)}, f32[16,4]{1,0:T(8,128)S(1)}, u32[]{:S(2)}, u32[]{:S(2)}) collective-permute-start(f32[16,4]{1,0:T(8,128)S(1)} %get-tuple-element.35), channel_id=1, source_target_pairs={{0,1},{1,2},{2,3},{3,4},{4,5},{5,6},{6,7},{7,8},{8,9},{9,10},{10,1... | collective-permute-start | bytes 776 | tf_op jit(solution)/shard_map/ppermute | solution.py:23
  67.3 6.8 %collective-permute-start.3 = (f32[16,4]{1,0:T(8,128)S(1)}, f32[16,4]{1,0:T(8,128)S(1)}, u32[]{:S(2)}, u32[]{:S(2)}) collective-permute-start(f32[16,4]{1,0:T(8,128)S(1)} %get-tuple-element.36), channel_id=1, source_target_pairs={{1,0},{2,1},{3,2},{4,3},{5,4},{6,5},{7,6},{8,7},{9,8},{10,9},{11,1... | collective-permute-start | bytes 776 | tf_op jit(solution)/shard_map/ppermute | solution.py:24
  74.5 22.6 %copy-start.8 = (f32[8,128]{1,0:T(8,128)}, f32[8,128]{1,0:T(8,128)S(1)}, u32[]{:S(2)}) copy-start(f32[8,128]{1,0:T(8,128)S(1)} %get-tuple-element.15) | copy-start | bytes 12292
  76.0 22.3 %copy-start.6 = (f32[64,8,128]{2,1,0:T(8,128)S(1)}, f32[64,8,128]{2,1,0:T(8,128)}, u32[]{:S(2)}) copy-start(f32[64,8,128]{2,1,0:T(8,128)} %get-tuple-element.12) | copy-start | bytes 786436
  97.1 0.7 copy-start.7

commit v4 on v3

--- a/solution.py
+++ b/solution.py
@@ -20,9 +20,11 @@
     count = lax.axis_size("aq")
     forward = [(i, i + 1) for i in range(count - 1)]
     backward = [(target, source) for source, target in forward]
-    low = lax.ppermute(block[..., block.shape[-1] - width:], "aq", forward)
-    high = lax.ppermute(block[..., :width], "aq", backward)
-    return jnp.concatenate([low, block, high], axis=-1)
+    low = lax.ppermute(jnp.swapaxes(block[..., block.shape[-1] - width:], -1, -2), "aq", forward)
+    high = lax.ppermute(jnp.swapaxes(block[..., :width], -1, -2), "aq", backward)
+    return jnp.concatenate(
+        [jnp.swapaxes(low, -1, -2), block, jnp.swapaxes(high, -1, -2)], axis=-1
+    )
 
 
 def column_kernel(
@@ -126,55 +128,91 @@
     return estimate
 
 
-def exchange_kernel(count, chunks_ref, out_ref, recv, send_sem, recv_sem):
+def exchange_kernel(planes, chunks_ref, out_ref, partial, recv_a, recv_b, send_a, got_a, send_b, got_b):
+    groups = chunks_ref.shape[0]
     me = lax.axis_index("long")
     column = lax.axis_index("aq")
+    my_core = lax.rem(me, 2)
+    my_plane = lax.rem(me // 2, planes)
+    my_group = (me // (2 * planes)) * 2 + my_core
+
+    def long_of(group, plane):
+        return (group // 2) * (2 * planes) + 2 * plane + lax.rem(group, 2)
+
+    peers_a = [long_of(lax.rem(my_group + k, groups), my_plane) for k in range(1, groups)]
+    peers_b = [long_of(my_group, lax.rem(my_plane + k, planes)) for k in range(1, planes)]
     barrier = pltpu.get_barrier_semaphore()
-    for k in range(1, count):
-        pl.semaphore_signal(
-            barrier, inc=1, device_id=(lax.rem(me + k, count), column), device_id_type=MESH
-        )
-    pl.semaphore_wait(barrier, count - 1)
+    for peer in peers_a + peers_b:
+        pl.semaphore_signal(barrier, inc=1, device_id=(peer, column), device_id_type=MESH)
+    pl.semaphore_wait(barrier, len(peers_a) + len(peers_b))
     copies = []
-    for k in range(1, count):
-        peer = lax.rem(me + k, count)
+    for k in range(1, groups):
         copy = pltpu.make_async_remote_copy(
-            src_ref=chunks_ref.at[peer],
-            dst_ref=recv.at[k],
-            send_sem=send_sem.at[k],
-            recv_sem=recv_sem.at[k],
-            device_id=(peer, column),
+            src_ref=chunks_ref.at[lax.rem(my_group + k, groups)],
+            dst_ref=recv_a.at[k],
+            send_sem=send_a.at[k],
+            recv_sem=got_a.at[k],
+            device_id=(peers_a[k - 1], column),
             device_id_type=MESH,
         )
         copy.start()
         copies.append(copy)
-    total = chunks_ref[me]
-    for k in range(1, count):
+    acc = chunks_ref[my_group]
+    for k in range(1, groups):
         copies[k - 1].wait()
-        total = total + recv[k]
+        acc = acc + recv_a[k]
+    partial[...] = acc
+    copies = []
+    for k in range(1, planes):
+        copy = pltpu.make_async_remote_copy(
+            src_ref=partial.at[lax.rem(my_plane + k, planes)],
+            dst_ref=recv_b.at[k],
+            send_sem=send_b.at[k],
+            recv_sem=got_b.at[k],
+            device_id=(peers_b[k - 1], column),
+            device_id_type=MESH,
+        )
+        copy.start()
+        copies.append(copy)
+    total = partial[my_plane]
+    for k in range(1, planes):
+        copies[k - 1].wait()
+        total = total + recv_b[k]
     out_ref[...] = total
+
+
+PLANES = 4
 
 
 def reduce_rows(term, wells, window, step, collective_id):
     count = lax.axis_size("long")
+    planes = PLANES
+    groups = count // planes
     cols = term.shape[1]
     edge = (window - step) // 2
     flat_wells = wells.reshape(1, -1)
     slot = lax.broadcasted_iota(jnp.int32, (count * window, 1), 0)
-    target_row = (slot // window) * step - edge + slot % window
+    group = slot // (planes * window)
+    plane = (slot // window) % planes
+    owner = (group // 2) * (2 * planes) + 2 * plane + group % 2
+    target_row = owner * step - edge + slot % window
     spread = jnp.where(flat_wells // cols == target_row, term.reshape(1, -1), 0.0)
     picks = flat_wells.reshape(-1, 1) % cols == lax.broadcasted_iota(jnp.int32, (1, cols), 1)
     chunks = jnp.dot(spread, picks.astype(jnp.float32), precision=lax.Precision.HIGHEST)
-    chunks = chunks.reshape(count, window, cols)
+    chunks = chunks.reshape(groups, planes, window, cols)
     return pl.pallas_call(
-        functools.partial(exchange_kernel, count),
+        functools.partial(exchange_kernel, planes),
         out_shape=jax.ShapeDtypeStruct((window, cols), jnp.float32),
         in_specs=[pl.BlockSpec(memory_space=pltpu.VMEM)],
         out_specs=pl.BlockSpec(memory_space=pltpu.VMEM),
         scratch_shapes=[
-            pltpu.VMEM((count, window, cols), jnp.float32),
-            pltpu.SemaphoreType.DMA((count,)),
-            pltpu.SemaphoreType.DMA((count,)),
+            pltpu.VMEM((planes, window, cols), jnp.float32),
+            pltpu.VMEM((groups, planes, window, cols), jnp.float32),
+            pltpu.VMEM((planes, window, cols), jnp.float32),
+            pltpu.SemaphoreType.DMA((groups,)),
+            pltpu.SemaphoreType.DMA((groups,)),
+            pltpu.SemaphoreType.DMA((planes,)),
+            pltpu.SemaphoreType.DMA((planes,)),
         ],
         compiler_params=pltpu.CompilerParams(collective_id=collective_id, has_side_effects=True),
     )(chunks)

time: 99.6 us -> 91.4 us (0.918)
  the two profiles are of different devices: /device:TPU:5 before, /device:TPU:96 now
where the time goes in v4:
time: 91.4 us; the launch traced here: 91 us
  Pallas kernels  47.8 us (52%)
  waiting for transfers between devices  18 us (20%)
  starting transfers between devices  13.5 us (15%)
  other arithmetic  5.65 us (6%)
  matrix products  3.46 us (4%)
  local copies, waits for them, and re-layouts  1.64 us (2%)
    pallas_call x2, Pallas kernels, reduce_rows(): pl.pallas_call(functools.partial(exchange_kernel, planes), out_shape=jax....  44.2 us
    ppermute x2, waiting for transfers between devices, aq_halo(): lax.ppermute(jnp.swapaxes(block[..., :width], -1, -2), 'aq', backward)  14.9 us
    ppermute x2, starting transfers between devices, aq_halo(): lax.ppermute(jnp.swapaxes(block[..., block.shape[-1] - width:], -1, -2),...  7.75 us
    ppermute x2, starting transfers between devices, aq_halo(): lax.ppermute(jnp.swapaxes(block[..., :width], -1, -2), 'aq', backward)  5.73 us
    pallas_call x1, Pallas kernels, column_solves(): pl.pallas_call(column_kernel, out_shape=(full, full, full, full, full, ja...  3.69 us
    dot_general x2, matrix products, reduce_rows(): jnp.dot(spread, picks.astype(jnp.float32), precision=lax.Precision.HIGHEST)  3.46 us
    ppermute x2, waiting for transfers between devices, aq_halo(): lax.ppermute(jnp.swapaxes(block[..., block.shape[-1] - width:], -1, -2),...  3.09 us
  transfers between devices with their start and end apart: 4, of which 3 were waited for; matrix products, arithmetic and copies ran while one was open for 0% of the time, Pallas kernels for 4%

profile of v4, /device:TPU:96, one launch (start us, length us, event | category | flops | bytes accessed | tf_op | source)
XLA Modules:
  0.0 91.0 jit_solution(7919981991891136894)
XLA Ops:
  0.6 1.1 %pad_maximum_fusion.1 = f32[3,256,128]{2,1,0:T(8,128)S(1)} fusion(f32[1,256,128]{2,1,0:T(8,128)} %bitcast.96, f32[1,256,128]{2,1,0:T(8,128)} %bitcast.98, f32[1,256,128]{2,1,0:T(8,128)} %bitcast.100), kind=kLoop, calls=%fused_computation.29 | loop fusion | flops 196608 | bytes 786432 | tf_op jit(solution)/shard_map/stack | solution.py:233
  1.7 0.0 copy-start.9
  1.7 0.2 slice_bitcast_fusion.1
  1.9 0.0 copy-start
  1.9 0.0 copy-start.1
  1.9 0.0 copy-start.2
  1.9 2.2 %collective-permute-start = (f32[3,4,256]{1,2,0:T(8,128)S(1)}, f32[3,4,256]{1,2,0:T(8,128)S(1)}, u32[]{:S(2)}, u32[]{:S(2)}) collective-permute-start(f32[3,4,256]{1,2,0:T(8,128)S(1)} %get-tuple-element.29), channel_id=1, source_target_pairs={{0,1},{1,2},{2,3},{3,4},{4,5},{5,6},{6,7},{7,8},{8,9},{9,10},{10,1... | collective-permute-start | bytes 36872 | tf_op jit(solution)/shard_map/ppermute | solution.py:23
  4.1 3.8 %collective-permute-start.1 = (f32[3,4,256]{1,2,0:T(8,128)S(1)}, f32[3,4,256]{1,2,0:T(8,128)S(1)}, u32[]{:S(2)}, u32[]{:S(2)}) collective-permute-start(f32[3,4,256]{1,2,0:T(8,128)S(1)} %get-tuple-element.30), channel_id=1, source_target_pairs={{1,0},{2,1},{3,2},{4,3},{5,4},{6,5},{7,6},{8,7},{9,8},{10,9},{11,1... | collective-permute-start | bytes 36872 | tf_op jit(solution)/shard_map/ppermute | solution.py:24
  8.0 0.0 copy-done.9
  8.0 3.7 %shard_map.112 = (f32[64,8,128]{2,1,0:T(8,128)}, f32[64,8,128]{2,1,0:T(8,128)}, f32[64,8,128]{2,1,0:T(8,128)}, f32[64,8,128]{2,1,0:T(8,128)}, f32[64,8,128]{2,1,0:T(8,128)}, /*index=5*/f32[8,128]{1,0:T(8,128)}) custom-call(f32[3,12]{1,0:T(4,128)} %table.1, s32[64,8,128]{2,1,0:T(8,128)} %tex.1, f32[2,64,8,128]{3,2,1,0:T(8,128)} %seed.1), custom_call_target="tpu_custom_call" | custom-call | tf_op jit(solution)/shard_map/pallas_call | solution.py:111
  11.7 3.1 %collective-permute-done = f32[3,4,256]{1,2,0:T(8,128)S(1)} collective-permute-done((f32[3,4,256]{1,2,0:T(8,128)S(1)}, f32[3,4,256]{1,2,0:T(8,128)S(1)}, u32[]{:S(2)}, u32[]{:S(2)}) %collective-permute-start) | collective-permute-done | bytes 12320 | tf_op jit(solution)/shard_map/ppermute | solution.py:23
  14.8 8.6 %collective-permute-done.1 = f32[3,4,256]{1,2,0:T(8,128)S(1)} collective-permute-done((f32[3,4,256]{1,2,0:T(8,128)S(1)}, f32[3,4,256]{1,2,0:T(8,128)S(1)}, u32[]{:S(2)}, u32[]{:S(2)}) %collective-permute-start.1) | collective-permute-done | bytes 12320 | tf_op jit(solution)/shard_map/ppermute | solution.py:24
  23.4 0.0 copy-done
  23.4 0.0 copy-done.1
  23.4 0.0 copy-done.2
  23.4 0.4 select_maximum_fusion
  23.9 0.6 fusion.22
  24.5 0.3 divide_add_fusion.1
  24.7 0.3 divide_add_fusion
  25.0 0.0 copy-start.3
  25.0 0.0 copy-start.10
  25.1 0.0 copy-start.11
  25.1 0.0 copy-start.12
  25.1 0.2 multiply_add_fusion
  25.3 0.7 copy-done.3
  26.0 0.0 copy-done.10
  26.0 0.0 copy-done.11
  26.0 0.0 copy-done.12
  26.0 0.1 fusion.98
  26.1 2.0 %fusion = f32[512,128]{1,0:T(8,128)} fusion(f32[1024]{0:T(1024)S(1)} %get-tuple-element.18, s32[1024]{0:T(1024)S(1)} %get-tuple-element.38, s32[512]{0:T(512)S(1)} %fusion.107, s32[1024]{0:T(1024)S(1)} %get-tuple-element.37), kind=kOutput, calls=%fused_computation | convolution fusion | flops 806486016 | bytes 276480 | tf_op jit(solution)/shard_map/dot_general | solution.py:201
  28.1 0.0 copy-start.4
  28.1 0.0 copy-start.5
  28.1 25.6 %shard_map.113 = f32[16,128]{1,0:T(8,128)} custom-call(f32[8,4,16,128]{3,2,1,0:T(8,128)} %bitcast.104), custom_call_target="tpu_custom_call" | custom-call | tf_op jit(solution)/shard_map/pallas_call | solution.py:203
  53.7 0.8 slice_add_fusion
  54.5 0.1 slice_bitcast_fusion.6
  54.5 5.6 %collective-permute-start.2 = (f32[4,16]{0,1:T(8,128)S(1)}, f32[4,16]{0,1:T(8,128)S(1)}, u32[]{:S(2)}, u32[]{:S(2)}) collective-permute-start(f32[4,16]{0,1:T(8,128)S(1)} %get-tuple-element.35), channel_id=1, source_target_pairs={{0,1},{1,2},{2,3},{3,4},{4,5},{5,6},{6,7},{7,8},{8,9},{9,10},{10,1... | collective-permute-start | bytes 776 | tf_op jit(solution)/shard_map/ppermute | solution.py:23
  60.1 1.9 %collective-permute-start.3 = (f32[4,16]{0,1:T(8,128)S(1)}, f32[4,16]{0,1:T(8,128)S(1)}, u32[]{:S(2)}, u32[]{:S(2)}) collective-permute-start(f32[4,16]{0,1:T(8,128)S(1)} %get-tuple-element.36), channel_id=1, source_target_pairs={{1,0},{2,1},{3,2},{4,3},{5,4},{6,5},{7,6},{8,7},{9,8},{10,9},{11,1... | collective-permute-start | bytes 776 | tf_op jit(solution)/shard_map/ppermute | solution.py:24
  62.1 0.0 collective-permute-done.2
  62.1 6.3 %collective-permute-done.3 = f32[4,16]{0,1:T(8,128)S(1)} collective-permute-done((f32[4,16]{0,1:T(8,128)S(1)}, f32[4,16]{0,1:T(8,128)S(1)}, u32[]{:S(2)}, u32[]{:S(2)}) %collective-permute-start.3) | collective-permute-done | bytes 288 | tf_op jit(solution)/shard_map/ppermute | solution.py:24
  68.4 0.1 fusion.76
  68.5 0.1 fusion.47
  68.5 0.1 fusion.59
  68.6 0.1 fusion.65
  68.7 0.0 copy-done.4
  68.7 0.0 copy-done.5
  68.7 0.1 fusion.95
  68.8 0.0 copy-start.8
  68.8 1.5 %fusion.3 = f32[256,128]{1,0:T(8,128)} fusion(f32[1024]{0:T(1024)S(1)} %get-tuple-element.13, s32[1024]{0:T(1024)S(1)} %get-tuple-element.38, s32[256]{0:T(256)S(1)} %fusion.125, s32[1024]{0:T(1024)S(1)} %get-tuple-element.37), kind=kOutput, calls=%fused_computation.5 | convolution fusion | flops 403308544 | bytes 144384 | tf_op jit(solution)/shard_map/dot_general | solution.py:201
  70.3 0.0 copy-start.6
  70.3 18.6 %shard_map.114 = f32[8,128]{1,0:T(8,128)} custom-call(f32[8,4,8,128]{3,2,1,0:T(8,128)} %bitcast.106), custom_call_target="tpu_custom_call" | custom-call | tf_op jit(solution)/shard_map/pallas_call | solution.py:203
  88.9 0.0 copy-start.7
  88.9 0.0 copy-done.8
  88.9 0.6 copy-done.7
  89.5 0.6 add.415
  90.1 0.0 copy-done.6
  90.1 0.8 pad_maximum_fusion
  (12 shorter events, 0.2 us)
Async XLA Ops:
  1.7 6.3 %copy-start.9 = (s32[8,128]{1,0:T(8,128)S(1)}, s32[8,128]{1,0:T(8,128)}, u32[]{:S(2)}) copy-start(s32[8,128]{1,0:T(8,128)} %param.15) | copy-start | bytes 12292
  1.9 21.5 %copy-start = (f32[256,128]{1,0:T(8,128)S(1)}, f32[256,128]{1,0:T(8,128)}, u32[]{:S(2)}) copy-start(f32[256,128]{1,0:T(8,128)} %param.17) | copy-start | bytes 393220
  1.9 21.5 %copy-start.1 = (f32[256,128]{1,0:T(8,128)S(1)}, f32[256,128]{1,0:T(8,128)}, u32[]{:S(2)}) copy-start(f32[256,128]{1,0:T(8,128)} %param.16) | copy-start | bytes 393220
  1.9 21.5 %copy-start.2 = (f32[256,128]{1,0:T(8,128)S(1)}, f32[256,128]{1,0:T(8,128)}, u32[]{:S(2)}) copy-start(f32[256,128]{1,0:T(8,128)} %param.10) | copy-start | bytes 393220
  1.9 12.9 %collective-permute-start = (f32[3,4,256]{1,2,0:T(8,128)S(1)}, f32[3,4,256]{1,2,0:T(8,128)S(1)}, u32[]{:S(2)}, u32[]{:S(2)}) collective-permute-start(f32[3,4,256]{1,2,0:T(8,128)S(1)} %get-tuple-element.29), channel_id=1, source_target_pairs={{0,1},{1,2},{2,3},{3,4},{4,5},{5,6},{6,7},{7,8},{8,9},{9,10},{10,1... | collective-permute-start | bytes 36872 | tf_op jit(solution)/shard_map/ppermute | solution.py:23
  4.1 19.3 %collective-permute-start.1 = (f32[3,4,256]{1,2,0:T(8,128)S(1)}, f32[3,4,256]{1,2,0:T(8,128)S(1)}, u32[]{:S(2)}, u32[]{:S(2)}) collective-permute-start(f32[3,4,256]{1,2,0:T(8,128)S(1)} %get-tuple-element.30), channel_id=1, source_target_pairs={{1,0},{2,1},{3,2},{4,3},{5,4},{6,5},{7,6},{8,7},{9,8},{10,9},{11,1... | collective-permute-start | bytes 36872 | tf_op jit(solution)/shard_map/ppermute | solution.py:24
  25.0 1.0 %copy-start.3 = (f32[64,8,128]{2,1,0:T(8,128)S(1)}, f32[64,8,128]{2,1,0:T(8,128)}, u32[]{:S(2)}) copy-start(f32[64,8,128]{2,1,0:T(8,128)} %get-tuple-element.11) | copy-start | bytes 786436
  25.0 0.9 %copy-start.10 = (f32[8,128]{1,0:T(8,128)S(1)}, f32[8,128]{1,0:T(8,128)}, u32[]{:S(2)}) copy-start(f32[8,128]{1,0:T(8,128)} %param.14) | copy-start | bytes 12292
  25.1 0.9 %copy-start.11 = (s32[8,128]{1,0:T(8,128)S(1)}, s32[8,128]{1,0:T(8,128)}, u32[]{:S(2)}) copy-start(s32[8,128]{1,0:T(8,128)} %param.13) | copy-start | bytes 12292
  25.1 0.9 %copy-start.12 = (f32[8,128]{1,0:T(8,128)S(1)}, f32[8,128]{1,0:T(8,128)}, u32[]{:S(2)}) copy-start(f32[8,128]{1,0:T(8,128)} %get-tuple-element.10) | copy-start | bytes 12292
  28.1 40.6 %copy-start.4 = (f32[64,8,128]{2,1,0:T(8,128)S(1)}, f32[64,8,128]{2,1,0:T(8,128)}, u32[]{:S(2)}) copy-start(f32[64,8,128]{2,1,0:T(8,128)} %get-tuple-element.8) | copy-start | bytes 786436
  28.1 40.6 %copy-start.5 = (f32[64,8,128]{2,1,0:T(8,128)S(1)}, f32[64,8,128]{2,1,0:T(8,128)}, u32[]{:S(2)}) copy-start(f32[64,8,128]{2,1,0:T(8,128)} %get-tuple-element.9) | copy-start | bytes 786436
  54.5 7.5 %collective-permute-start.2 = (f32[4,16]{0,1:T(8,128)S(1)}, f32[4,16]{0,1:T(8,128)S(1)}, u32[]{:S(2)}, u32[]{:S(2)}) collective-permute-start(f32[4,16]{0,1:T(8,128)S(1)} %get-tuple-element.35), channel_id=1, source_target_pairs={{0,1},{1,2},{2,3},{3,4},{4,5},{5,6},{6,7},{7,8},{8,9},{9,10},{10,1... | collective-permute-start | bytes 776 | tf_op jit(solution)/shard_map/ppermute | solution.py:23
  60.1 8.2 %collective-permute-start.3 = (f32[4,16]{0,1:T(8,128)S(1)}, f32[4,16]{0,1:T(8,128)S(1)}, u32[]{:S(2)}, u32[]{:S(2)}) collective-permute-start(f32[4,16]{0,1:T(8,128)S(1)} %get-tuple-element.36), channel_id=1, source_target_pairs={{1,0},{2,1},{3,2},{4,3},{5,4},{6,5},{7,6},{8,7},{9,8},{10,9},{11,1... | collective-permute-start | bytes 776 | tf_op jit(solution)/shard_map/ppermute | solution.py:24
  68.8 20.1 %copy-start.8 = (f32[8,128]{1,0:T(8,128)}, f32[8,128]{1,0:T(8,128)S(1)}, u32[]{:S(2)}) copy-start(f32[8,128]{1,0:T(8,128)S(1)} %get-tuple-element.15) | copy-start | bytes 12292
  70.3 19.9 %copy-start.6 = (f32[64,8,128]{2,1,0:T(8,128)S(1)}, f32[64,8,128]{2,1,0:T(8,128)}, u32[]{:S(2)}) copy-start(f32[64,8,128]{2,1,0:T(8,128)} %get-tuple-element.12) | copy-start | bytes 786436
  88.9 0.7 copy-start.7

commit v5 on v4

--- a/solution.py
+++ b/solution.py
@@ -198,7 +198,7 @@
     target_row = owner * step - edge + slot % window
     spread = jnp.where(flat_wells // cols == target_row, term.reshape(1, -1), 0.0)
     picks = flat_wells.reshape(-1, 1) % cols == lax.broadcasted_iota(jnp.int32, (1, cols), 1)
-    chunks = jnp.dot(spread, picks.astype(jnp.float32), precision=lax.Precision.HIGHEST)
+    chunks = jnp.dot(spread, picks.astype(jnp.float32), precision=lax.Precision.HIGH)
     chunks = chunks.reshape(groups, planes, window, cols)
     return pl.pallas_call(
         functools.partial(exchange_kernel, planes),

time: 91.4 us -> 90.6 us (level)
  no operation moved by 1% of the time
where the time goes in v5:
time: 90.6 us; the launch traced here: 90.2 us
  Pallas kernels  47.8 us (53%)
  waiting for transfers between devices  18 us (20%)
  starting transfers between devices  13.5 us (15%)
  other arithmetic  5.65 us (6%)
  matrix products  2.68 us (3%)
  local copies, waits for them, and re-layouts  1.64 us (2%)
  between operations  0.91 us (1%)
    pallas_call x2, Pallas kernels, reduce_rows(): pl.pallas_call(functools.partial(exchange_kernel, planes), out_shape=jax....  44.2 us
    ppermute x2, waiting for transfers between devices, aq_halo(): lax.ppermute(jnp.swapaxes(block[..., :width], -1, -2), 'aq', backward)  14.9 us
    ppermute x2, starting transfers between devices, aq_halo(): lax.ppermute(jnp.swapaxes(block[..., block.shape[-1] - width:], -1, -2),...  7.75 us
    ppermute x2, starting transfers between devices, aq_halo(): lax.ppermute(jnp.swapaxes(block[..., :width], -1, -2), 'aq', backward)  5.73 us
    pallas_call x1, Pallas kernels, column_solves(): pl.pallas_call(column_kernel, out_shape=(full, full, full, full, full, ja...  3.69 us
    ppermute x2, waiting for transfers between devices, aq_halo(): lax.ppermute(jnp.swapaxes(block[..., block.shape[-1] - width:], -1, -2),...  3.09 us
    dot_general x2, matrix products, reduce_rows(): jnp.dot(spread, picks.astype(jnp.float32), precision=lax.Precision.HIGH)  2.68 us
  transfers between devices with their start and end apart: 4, of which 3 were waited for; matrix products, arithmetic and copies ran while one was open for 0% of the time, Pallas kernels for 4%

profile of v5, /device:TPU:96, one launch (start us, length us, event | category | flops | bytes accessed | tf_op | source)
XLA Modules:
  0.0 90.2 jit_solution(8342244203385237199)
XLA Ops:
  0.6 1.1 %pad_maximum_fusion.1 = f32[3,256,128]{2,1,0:T(8,128)S(1)} fusion(f32[1,256,128]{2,1,0:T(8,128)} %bitcast.96, f32[1,256,128]{2,1,0:T(8,128)} %bitcast.98, f32[1,256,128]{2,1,0:T(8,128)} %bitcast.100), kind=kLoop, calls=%fused_computation.29 | loop fusion | flops 196608 | bytes 786432 | tf_op jit(solution)/shard_map/stack | solution.py:233
  1.7 0.0 copy-start.9
  1.7 0.2 slice_bitcast_fusion.1
  1.9 0.0 copy-start
  1.9 0.0 copy-start.1
  1.9 0.0 copy-start.2
  1.9 2.2 %collective-permute-start = (f32[3,4,256]{1,2,0:T(8,128)S(1)}, f32[3,4,256]{1,2,0:T(8,128)S(1)}, u32[]{:S(2)}, u32[]{:S(2)}) collective-permute-start(f32[3,4,256]{1,2,0:T(8,128)S(1)} %get-tuple-element.29), channel_id=1, source_target_pairs={{0,1},{1,2},{2,3},{3,4},{4,5},{5,6},{6,7},{7,8},{8,9},{9,10},{10,1... | collective-permute-start | bytes 36872 | tf_op jit(solution)/shard_map/ppermute | solution.py:23
  4.1 3.8 %collective-permute-start.1 = (f32[3,4,256]{1,2,0:T(8,128)S(1)}, f32[3,4,256]{1,2,0:T(8,128)S(1)}, u32[]{:S(2)}, u32[]{:S(2)}) collective-permute-start(f32[3,4,256]{1,2,0:T(8,128)S(1)} %get-tuple-element.30), channel_id=1, source_target_pairs={{1,0},{2,1},{3,2},{4,3},{5,4},{6,5},{7,6},{8,7},{9,8},{10,9},{11,1... | collective-permute-start | bytes 36872 | tf_op jit(solution)/shard_map/ppermute | solution.py:24
  8.0 0.0 copy-done.9
  8.0 3.7 %shard_map.112 = (f32[64,8,128]{2,1,0:T(8,128)}, f32[64,8,128]{2,1,0:T(8,128)}, f32[64,8,128]{2,1,0:T(8,128)}, f32[64,8,128]{2,1,0:T(8,128)}, f32[64,8,128]{2,1,0:T(8,128)}, /*index=5*/f32[8,128]{1,0:T(8,128)}) custom-call(f32[3,12]{1,0:T(4,128)} %table.1, s32[64,8,128]{2,1,0:T(8,128)} %tex.1, f32[2,64,8,128]{3,2,1,0:T(8,128)} %seed.1), custom_call_target="tpu_custom_call" | custom-call | tf_op jit(solution)/shard_map/pallas_call | solution.py:111
  11.7 3.1 %collective-permute-done = f32[3,4,256]{1,2,0:T(8,128)S(1)} collective-permute-done((f32[3,4,256]{1,2,0:T(8,128)S(1)}, f32[3,4,256]{1,2,0:T(8,128)S(1)}, u32[]{:S(2)}, u32[]{:S(2)}) %collective-permute-start) | collective-permute-done | bytes 12320 | tf_op jit(solution)/shard_map/ppermute | solution.py:23
  14.8 8.6 %collective-permute-done.1 = f32[3,4,256]{1,2,0:T(8,128)S(1)} collective-permute-done((f32[3,4,256]{1,2,0:T(8,128)S(1)}, f32[3,4,256]{1,2,0:T(8,128)S(1)}, u32[]{:S(2)}, u32[]{:S(2)}) %collective-permute-start.1) | collective-permute-done | bytes 12320 | tf_op jit(solution)/shard_map/ppermute | solution.py:24
  23.4 0.0 copy-done
  23.4 0.0 copy-done.1
  23.4 0.0 copy-done.2
  23.4 0.4 select_maximum_fusion
  23.9 0.6 fusion.22
  24.5 0.3 divide_add_fusion.1
  24.7 0.3 divide_add_fusion
  25.0 0.0 copy-start.3
  25.0 0.0 copy-start.10
  25.1 0.0 copy-start.11
  25.1 0.0 copy-start.12
  25.1 0.2 multiply_add_fusion
  25.3 0.7 copy-done.3
  26.0 0.0 copy-done.10
  26.0 0.0 copy-done.11
  26.0 0.0 copy-done.12
  26.0 0.1 fusion.98
  26.1 1.5 %fusion = f32[512,128]{1,0:T(8,128)} fusion(f32[1024]{0:T(1024)S(1)} %get-tuple-element.18, s32[1024]{0:T(1024)S(1)} %get-tuple-element.38, s32[512]{0:T(512)S(1)} %fusion.107, s32[1024]{0:T(1024)S(1)} %get-tuple-element.37), kind=kOutput, calls=%fused_computation | convolution fusion | flops 403832832 | bytes 276480 | tf_op jit(solution)/shard_map/dot_general | solution.py:201
  27.6 0.0 copy-start.4
  27.6 0.0 copy-start.5
  27.6 25.6 %shard_map.113 = f32[16,128]{1,0:T(8,128)} custom-call(f32[8,4,16,128]{3,2,1,0:T(8,128)} %bitcast.104), custom_call_target="tpu_custom_call" | custom-call | tf_op jit(solution)/shard_map/pallas_call | solution.py:203
  53.2 0.8 slice_add_fusion
  53.9 0.1 slice_bitcast_fusion.6
  54.0 5.6 %collective-permute-start.2 = (f32[4,16]{0,1:T(8,128)S(1)}, f32[4,16]{0,1:T(8,128)S(1)}, u32[]{:S(2)}, u32[]{:S(2)}) collective-permute-start(f32[4,16]{0,1:T(8,128)S(1)} %get-tuple-element.35), channel_id=1, source_target_pairs={{0,1},{1,2},{2,3},{3,4},{4,5},{5,6},{6,7},{7,8},{8,9},{9,10},{10,1... | collective-permute-start | bytes 776 | tf_op jit(solution)/shard_map/ppermute | solution.py:23
  59.6 1.9 %collective-permute-start.3 = (f32[4,16]{0,1:T(8,128)S(1)}, f32[4,16]{0,1:T(8,128)S(1)}, u32[]{:S(2)}, u32[]{:S(2)}) collective-permute-start(f32[4,16]{0,1:T(8,128)S(1)} %get-tuple-element.36), channel_id=1, source_target_pairs={{1,0},{2,1},{3,2},{4,3},{5,4},{6,5},{7,6},{8,7},{9,8},{10,9},{11,1... | collective-permute-start | bytes 776 | tf_op jit(solution)/shard_map/ppermute | solution.py:24
  61.6 0.0 collective-permute-done.2
  61.6 6.3 %collective-permute-done.3 = f32[4,16]{0,1:T(8,128)S(1)} collective-permute-done((f32[4,16]{0,1:T(8,128)S(1)}, f32[4,16]{0,1:T(8,128)S(1)}, u32[]{:S(2)}, u32[]{:S(2)}) %collective-permute-start.3) | collective-permute-done | bytes 288 | tf_op jit(solution)/shard_map/ppermute | solution.py:24
  67.9 0.1 fusion.76
  67.9 0.1 fusion.47
  68.0 0.1 fusion.59
  68.1 0.1 fusion.65
  68.2 0.0 copy-done.4
  68.2 0.0 copy-done.5
  68.2 0.1 fusion.95
  68.3 0.0 copy-start.8
  68.3 1.2 %fusion.3 = f32[256,128]{1,0:T(8,128)} fusion(f32[1024]{0:T(1024)S(1)} %get-tuple-element.13, s32[1024]{0:T(1024)S(1)} %get-tuple-element.38, s32[256]{0:T(256)S(1)} %fusion.125, s32[1024]{0:T(1024)S(1)} %get-tuple-element.37), kind=kOutput, calls=%fused_computation.5 | convolution fusion | flops 201981952 | bytes 144384 | tf_op jit(solution)/shard_map/dot_general | solution.py:201
  69.5 0.0 copy-start.6
  69.5 18.6 %shard_map.114 = f32[8,128]{1,0:T(8,128)} custom-call(f32[8,4,8,128]{3,2,1,0:T(8,128)} %bitcast.106), custom_call_target="tpu_custom_call" | custom-call | tf_op jit(solution)/shard_map/pallas_call | solution.py:203
  88.1 0.0 copy-start.7
  88.1 0.0 copy-done.8
  88.1 0.6 copy-done.7
  88.8 0.6 add.415
  89.3 0.0 copy-done.6
  89.4 0.8 pad_maximum_fusion
  (12 shorter events, 0.2 us)
Async XLA Ops:
  1.7 6.3 %copy-start.9 = (s32[8,128]{1,0:T(8,128)S(1)}, s32[8,128]{1,0:T(8,128)}, u32[]{:S(2)}) copy-start(s32[8,128]{1,0:T(8,128)} %param.15) | copy-start | bytes 12292
  1.9 21.5 %copy-start = (f32[256,128]{1,0:T(8,128)S(1)}, f32[256,128]{1,0:T(8,128)}, u32[]{:S(2)}) copy-start(f32[256,128]{1,0:T(8,128)} %param.17) | copy-start | bytes 393220
  1.9 21.5 %copy-start.1 = (f32[256,128]{1,0:T(8,128)S(1)}, f32[256,128]{1,0:T(8,128)}, u32[]{:S(2)}) copy-start(f32[256,128]{1,0:T(8,128)} %param.16) | copy-start | bytes 393220
  1.9 21.5 %copy-start.2 = (f32[256,128]{1,0:T(8,128)S(1)}, f32[256,128]{1,0:T(8,128)}, u32[]{:S(2)}) copy-start(f32[256,128]{1,0:T(8,128)} %param.10) | copy-start | bytes 393220
  1.9 12.9 %collective-permute-start = (f32[3,4,256]{1,2,0:T(8,128)S(1)}, f32[3,4,256]{1,2,0:T(8,128)S(1)}, u32[]{:S(2)}, u32[]{:S(2)}) collective-permute-start(f32[3,4,256]{1,2,0:T(8,128)S(1)} %get-tuple-element.29), channel_id=1, source_target_pairs={{0,1},{1,2},{2,3},{3,4},{4,5},{5,6},{6,7},{7,8},{8,9},{9,10},{10,1... | collective-permute-start | bytes 36872 | tf_op jit(solution)/shard_map/ppermute | solution.py:23
  4.1 19.3 %collective-permute-start.1 = (f32[3,4,256]{1,2,0:T(8,128)S(1)}, f32[3,4,256]{1,2,0:T(8,128)S(1)}, u32[]{:S(2)}, u32[]{:S(2)}) collective-permute-start(f32[3,4,256]{1,2,0:T(8,128)S(1)} %get-tuple-element.30), channel_id=1, source_target_pairs={{1,0},{2,1},{3,2},{4,3},{5,4},{6,5},{7,6},{8,7},{9,8},{10,9},{11,1... | collective-permute-start | bytes 36872 | tf_op jit(solution)/shard_map/ppermute | solution.py:24
  25.0 1.0 %copy-start.3 = (f32[64,8,128]{2,1,0:T(8,128)S(1)}, f32[64,8,128]{2,1,0:T(8,128)}, u32[]{:S(2)}) copy-start(f32[64,8,128]{2,1,0:T(8,128)} %get-tuple-element.11) | copy-start | bytes 786436
  25.0 0.9 %copy-start.10 = (f32[8,128]{1,0:T(8,128)S(1)}, f32[8,128]{1,0:T(8,128)}, u32[]{:S(2)}) copy-start(f32[8,128]{1,0:T(8,128)} %param.14) | copy-start | bytes 12292
  25.1 0.9 %copy-start.11 = (s32[8,128]{1,0:T(8,128)S(1)}, s32[8,128]{1,0:T(8,128)}, u32[]{:S(2)}) copy-start(s32[8,128]{1,0:T(8,128)} %param.13) | copy-start | bytes 12292
  25.1 0.9 %copy-start.12 = (f32[8,128]{1,0:T(8,128)S(1)}, f32[8,128]{1,0:T(8,128)}, u32[]{:S(2)}) copy-start(f32[8,128]{1,0:T(8,128)} %get-tuple-element.10) | copy-start | bytes 12292
  27.6 40.6 %copy-start.4 = (f32[64,8,128]{2,1,0:T(8,128)S(1)}, f32[64,8,128]{2,1,0:T(8,128)}, u32[]{:S(2)}) copy-start(f32[64,8,128]{2,1,0:T(8,128)} %get-tuple-element.8) | copy-start | bytes 786436
  27.6 40.6 %copy-start.5 = (f32[64,8,128]{2,1,0:T(8,128)S(1)}, f32[64,8,128]{2,1,0:T(8,128)}, u32[]{:S(2)}) copy-start(f32[64,8,128]{2,1,0:T(8,128)} %get-tuple-element.9) | copy-start | bytes 786436
  54.0 7.5 %collective-permute-start.2 = (f32[4,16]{0,1:T(8,128)S(1)}, f32[4,16]{0,1:T(8,128)S(1)}, u32[]{:S(2)}, u32[]{:S(2)}) collective-permute-start(f32[4,16]{0,1:T(8,128)S(1)} %get-tuple-element.35), channel_id=1, source_target_pairs={{0,1},{1,2},{2,3},{3,4},{4,5},{5,6},{6,7},{7,8},{8,9},{9,10},{10,1... | collective-permute-start | bytes 776 | tf_op jit(solution)/shard_map/ppermute | solution.py:23
  59.6 8.2 %collective-permute-start.3 = (f32[4,16]{0,1:T(8,128)S(1)}, f32[4,16]{0,1:T(8,128)S(1)}, u32[]{:S(2)}, u32[]{:S(2)}) collective-permute-start(f32[4,16]{0,1:T(8,128)S(1)} %get-tuple-element.36), channel_id=1, source_target_pairs={{1,0},{2,1},{3,2},{4,3},{5,4},{6,5},{7,6},{8,7},{9,8},{10,9},{11,1... | collective-permute-start | bytes 776 | tf_op jit(solution)/shard_map/ppermute | solution.py:24
  68.3 19.8 %copy-start.8 = (f32[8,128]{1,0:T(8,128)}, f32[8,128]{1,0:T(8,128)S(1)}, u32[]{:S(2)}) copy-start(f32[8,128]{1,0:T(8,128)S(1)} %get-tuple-element.15) | copy-start | bytes 12292
  69.5 19.9 %copy-start.6 = (f32[64,8,128]{2,1,0:T(8,128)S(1)}, f32[64,8,128]{2,1,0:T(8,128)}, u32[]{:S(2)}) copy-start(f32[64,8,128]{2,1,0:T(8,128)} %get-tuple-element.12) | copy-start | bytes 786436
  88.1 0.7 copy-start.7
